TPU v7x, 32 devices: a whole 2x2x4 slice. The times are simulated.
32 devices in a mesh: ctx: 8 (over y, x, core), ep: 4 (over z).
Axes of the slice: x: 2, y: 2, z: 4, core: 2. Of those that a mesh axis runs over, the one named last changes fastest.
Arguments:
- out_grad: bfloat16 [2048, 2048], P('ctx'), may hold values from -12 to 12
- gate_values: bfloat16 [2048, 8], P('ctx'), may hold values from 0.049804688 to 0.3984375
- expert_ids: int32 [2048, 8], P('ctx'), may hold values from 0 to 15, all different within a row; in each aligned block of 256 rows (0 to 255, 256 to 511, ...) at most 192 rows name the same one
- segment_ids: int32 [2048], P('ctx'), may hold values from 0 to 3, never falling along the last dimension, each value on 1 to 1793 neighbouring positions
- gate_pre: bfloat16 [32, 8, 192, 512], P(('ctx', 'ep')), may hold values from -6 to 6
- up_pre: bfloat16 [32, 8, 192, 512], P(('ctx', 'ep')), may hold values from -6 to 6
- w_gate: bfloat16 [32, 2048, 512], P(('ctx', 'ep')), may hold values from -0.125 to 0.125
- w_up: bfloat16 [32, 2048, 512], P(('ctx', 'ep')), may hold values from -0.125 to 0.125
- w_down: bfloat16 [32, 512, 2048], P(('ctx', 'ep')), may hold values from -0.1875 to 0.1875
- queries: bfloat16 [2048, 2048], P('ctx', 'ep'), may hold values from -0.015625 to 0.015625
- keys: bfloat16 [2048, 2048], P('ctx', 'ep'), may hold values from -0.015625 to 0.015625
- values: bfloat16 [2048, 2048], P('ctx', 'ep'), may hold values from -6 to 6
Outputs:
- query_grad: bfloat16 [2048, 2048], P('ctx', 'ep')
- key_grad: bfloat16 [2048, 2048], P('ctx', 'ep')
- value_grad: bfloat16 [2048, 2048], P('ctx', 'ep')
- down_grad: float32 [32, 512, 2048], P(('ctx', 'ep'))
Inputs may be any that keep to these rules, and one draw needn't show every extreme that they name: `expert_ids`: each token names 8 different experts. Among the 256 tokens of one context shard at most 192 name the same expert, and in every draw some shard has exactly 192 tokens that name one expert. `segment_ids`: document numbers never fall along the tokens; a document has 1 to 1793 tokens and one has exactly 1793, so that no document covers more than eight context shards of 256 tokens.
All inputs are finite; a program needn't handle non-finite values.
Results may differ from a plain program's by a relative error of at most 0.008.
Values may be sent and summed in bfloat16 or wider, within the bound.
No kernel may reach another device: no remote copies, remote signals or barrier semaphores. Data moves between devices by JAX's collectives and lax.ppermute only.
A program may use at most 128 MiB of HBM per device.

v0:
```python
import jax
import jax.numpy as jnp
from jax import lax
from jax.sharding import PartitionSpec as P

HEAD_DIM = 128


HIGHEST = lax.Precision.HIGHEST


def prefix(shard, axis, join, neutral, backward):
    count = lax.axis_size(axis)
    place = lax.axis_index(axis)
    ahead = count - 1 - place if backward else place
    gathered = jax.tree.map(
        lambda a, kind: lax.all_gather(a.astype(kind), axis),
        shard,
        jax.tree.map(lambda a: jnp.bfloat16 if a.dtype == jnp.float32 else a.dtype, shard),
    )
    state = jax.tree.map(lambda a, e: jnp.zeros_like(a) + jnp.asarray(e, a.dtype), shard, neutral)

    def one(hop, state):
        source = count - 1 - hop if backward else hop
        return join(
            state,
            jax.tree.map(
                lambda a, own: lax.dynamic_index_in_dim(a, source, 0, False).astype(own.dtype),
                gathered,
                shard,
            ),
        )

    return lax.fori_loop(0, ahead, one, state)


def count_before(flat_ids, expert_count):
    labels = jnp.arange(expert_count, dtype=jnp.int32)
    onehot = (flat_ids[:, None] == labels[None, :]).astype(jnp.int32)
    before = jnp.cumsum(onehot, axis=0) - onehot
    return jnp.sum(before * onehot, axis=1)


def expert_rows(cotangent, pre_gate, pre_up, gate_matrix, up_matrix, down_matrix):
    down_part = lax.dot_general(
        cotangent, down_matrix, (((1,), (1,)), ((), ())), preferred_element_type=jnp.float32
    )
    gate_value = pre_gate.astype(jnp.float32)
    up_value = pre_up.astype(jnp.float32)
    sigmoid_gate = jax.nn.sigmoid(gate_value)
    hidden = (gate_value * sigmoid_gate * up_value).astype(jnp.bfloat16)
    down_grad = lax.dot_general(
        hidden, cotangent, (((0,), (0,)), ((), ())), preferred_element_type=jnp.float32
    )
    gate_delta = (
        down_part * up_value * sigmoid_gate * (1.0 + gate_value * (1.0 - sigmoid_gate))
    ).astype(jnp.bfloat16)
    up_delta = (down_part * gate_value * sigmoid_gate).astype(jnp.bfloat16)
    input_part = lax.dot_general(
        gate_delta, gate_matrix, (((1,), (1,)), ((), ())), preferred_element_type=jnp.float32
    )
    input_part = input_part + lax.dot_general(
        up_delta, up_matrix, (((1,), (1,)), ((), ())), preferred_element_type=jnp.float32
    )
    return (input_part.astype(jnp.bfloat16), down_grad)


def gather_back(returned, owner_of, slot_rank, is_mine, offset, piece_slots, tok_rows, top_count):
    model_width = returned.shape[2]
    local_rank = slot_rank - offset
    usable = is_mine & (local_rank >= 0) & (local_rank < piece_slots)
    row_index = jnp.where(usable, owner_of * piece_slots + local_rank, 0)
    picked = jnp.take(returned.reshape(-1, model_width), row_index, axis=0).astype(jnp.float32)
    picked = picked * usable.astype(jnp.float32)[:, None]
    return jnp.sum(picked.reshape(tok_rows, top_count, model_width), axis=1)


def join_states(earlier, latter):
    state_a, doc_a, whole_a, filled_a = earlier
    state_b, doc_b, whole_b, filled_b = latter
    empty_a = filled_a == 0.0
    empty_b = filled_b == 0.0
    same_doc = doc_a == doc_b
    carried = empty_b | (whole_b > 0.0) & same_doc
    state_sum = state_b + jnp.where(carried[..., None, None, None], state_a, 0.0)
    doc_id = jnp.where(empty_b, doc_a, doc_b)
    joined = jnp.where((whole_a > 0.0) & (whole_b > 0.0) & same_doc, 1.0, 0.0)
    whole_doc = jnp.where(empty_b, whole_a, jnp.where(empty_a, whole_b, joined))
    return (state_sum, doc_id, whole_doc, jnp.maximum(filled_a, filled_b))


def within_block(query3, key3, value3, cot3, segment):
    positions = jnp.arange(segment.shape[0], dtype=jnp.int32)
    allowed = (
        (positions[:, None] >= positions[None, :]) & (segment[:, None] == segment[None, :])
    ).astype(jnp.float32)
    cot_value = (
        jnp.einsum("the,she->hts", cot3, value3, preferred_element_type=jnp.float32) * allowed[None]
    )
    query_key = (
        jnp.einsum("the,she->hts", query3, key3, preferred_element_type=jnp.float32) * allowed[None]
    )
    query_grad = jnp.einsum("hts,she->the", cot_value, key3.astype(jnp.float32), precision=HIGHEST)
    key_grad = jnp.einsum("hts,the->she", cot_value, query3.astype(jnp.float32), precision=HIGHEST)
    value_grad = jnp.einsum("hts,the->she", query_key, cot3.astype(jnp.float32), precision=HIGHEST)
    return (query_grad, key_grad, value_grad)


def end_states(query3, key3, value3, cot3, segment):
    last_mask = (segment == segment[-1])[:, None, None]
    first_mask = (segment == segment[0])[:, None, None]
    forward_state = jnp.einsum(
        "the,thf->hef",
        jnp.where(last_mask, key3, jnp.zeros_like(key3)),
        value3,
        preferred_element_type=jnp.float32,
    )
    backward_state = jnp.einsum(
        "the,thf->hef",
        jnp.where(first_mask, query3, jnp.zeros_like(query3)),
        cot3,
        preferred_element_type=jnp.float32,
    )
    return (forward_state, backward_state)


def across_blocks(key3, value3, cot3, before_mask, after_mask, state_in, back_in):
    query_part = (
        jnp.einsum("thf,hef->the", cot3.astype(jnp.float32), state_in, precision=HIGHEST)
        * before_mask
    )
    key_part = (
        jnp.einsum("thf,hef->the", value3.astype(jnp.float32), back_in, precision=HIGHEST)
        * after_mask
    )
    value_part = (
        jnp.einsum("the,hef->thf", key3.astype(jnp.float32), back_in, precision=HIGHEST)
        * after_mask
    )
    return (query_part, key_part, value_part)


def local(
    out_grad,
    gate_values,
    expert_ids,
    segment_ids,
    gate_pre,
    up_pre,
    w_gate,
    w_up,
    w_down,
    queries,
    keys,
    values,
):
    owners = lax.axis_size("ctx")
    groups = lax.axis_size("ep")
    part_count = groups // 2
    device_place = lax.axis_index("ep")
    parity = device_place // part_count
    tok_rows, model_width = out_grad.shape
    top_count = expert_ids.shape[1]
    slot_count = gate_pre.shape[2]
    flat_ids = expert_ids.reshape(-1)
    slot_rank = count_before(flat_ids, 2 * owners)
    owner_of = flat_ids // 2
    is_mine = flat_ids % 2 == parity
    token_of = jnp.arange(tok_rows * top_count, dtype=jnp.int32) // top_count
    dump_slot = owners * slot_count
    position = jnp.where(is_mine, owner_of * slot_count + slot_rank, dump_slot)
    slot_token = jnp.full((dump_slot,), tok_rows, jnp.int32).at[position].set(token_of, mode="drop")
    slot_gate = (
        jnp.zeros((dump_slot,), gate_values.dtype)
        .at[position]
        .set(gate_values.reshape(-1), mode="drop")
    )
    padded = jnp.concatenate([out_grad, jnp.zeros((1, model_width), out_grad.dtype)], axis=0)
    send_rows = jnp.take(padded, slot_token, axis=0).reshape(owners, slot_count, model_width)
    send_gates = slot_gate.reshape(owners, slot_count)
    pre_gate = gate_pre[0].reshape(dump_slot, -1)
    pre_up = up_pre[0].reshape(dump_slot, -1)
    got_rows, got_gates = (
        lax.all_to_all(send_rows, "ctx", split_axis=0, concat_axis=0, tiled=True),
        lax.all_to_all(send_gates, "ctx", split_axis=0, concat_axis=0, tiled=True),
    )
    cotangent = (got_gates[..., None].astype(jnp.float32) * got_rows.astype(jnp.float32)).astype(
        jnp.bfloat16
    )
    input_part, down_grad = expert_rows(
        cotangent.reshape(dump_slot, model_width), pre_gate, pre_up, w_gate[0], w_up[0], w_down[0]
    )
    returned = lax.all_to_all(
        input_part.reshape(owners, slot_count, model_width),
        "ctx",
        split_axis=0,
        concat_axis=0,
        tiled=True,
    )
    offset = 0
    token_sum = gather_back(
        returned, owner_of, slot_rank, is_mine, offset, slot_count, tok_rows, top_count
    )
    head_sum = lax.psum_scatter(token_sum, "ep", scatter_dimension=1, tiled=True)
    head_cot = head_sum.astype(jnp.bfloat16)
    heads_here = queries.shape[1] // HEAD_DIM
    head_shape = (tok_rows, heads_here, HEAD_DIM)
    query3 = queries.reshape(head_shape)
    key3 = keys.reshape(head_shape)
    value3 = values.reshape(head_shape)
    cot3 = head_cot.reshape(head_shape)
    inner_query, inner_key, inner_value = within_block(query3, key3, value3, cot3, segment_ids)
    forward_state, backward_state = end_states(query3, key3, value3, cot3, segment_ids)
    seg_float = segment_ids.astype(jnp.float32)
    whole_doc = (segment_ids[0] == segment_ids[-1]).astype(jnp.float32)
    filled = jnp.ones((), jnp.float32)
    forward_element = (forward_state, seg_float[-1], whole_doc, filled)
    backward_element = (backward_state, seg_float[0], whole_doc, filled)
    identity = (
        jnp.zeros_like(forward_state),
        jnp.full((), -1.0, jnp.float32),
        jnp.ones((), jnp.float32),
        jnp.zeros((), jnp.float32),
    )
    before = prefix(forward_element, "ctx", join_states, identity, False)
    following = prefix(backward_element, "ctx", join_states, identity, True)
    before_mask = (seg_float == before[1]).astype(jnp.float32)[:, None, None]
    after_mask = (seg_float == following[1]).astype(jnp.float32)[:, None, None]
    outer_query, outer_key, outer_value = across_blocks(
        key3, value3, cot3, before_mask, after_mask, before[0], following[0]
    )
    query_grad = (inner_query + outer_query).astype(jnp.bfloat16).reshape(tok_rows, -1)
    key_grad = (inner_key + outer_key).astype(jnp.bfloat16).reshape(tok_rows, -1)
    value_grad = (inner_value + outer_value).astype(jnp.bfloat16).reshape(tok_rows, -1)
    return (query_grad, key_grad, value_grad, down_grad[None])


def solution(mesh):
    return jax.shard_map(
        local,
        mesh=mesh,
        in_specs=(
            P("ctx", None),
            P("ctx", None),
            P("ctx", None),
            P("ctx"),
            P(("ctx", "ep"), None, None, None),
            P(("ctx", "ep"), None, None, None),
            P(("ctx", "ep"), None, None),
            P(("ctx", "ep"), None, None),
            P(("ctx", "ep"), None, None),
            P("ctx", "ep"),
            P("ctx", "ep"),
            P("ctx", "ep"),
        ),
        out_specs=(P("ctx", "ep"), P("ctx", "ep"), P("ctx", "ep"), P(("ctx", "ep"), None, None)),
        check_vma=False,
    )
```

profile of v0, /device:TPU:0, one launch (start us, length us, event | category | flops | bytes accessed | tf_op | source)
XLA Modules:
  0.0 392.0 jit_solution(7325847065765838518)
XLA Ops:
  9.4 4.5 %reduce-window.6 = s32[16,16,128]{2,1,0:T(8,128)S(1)} reduce-window(s32[16,16,128]{2,1,0:T(8,128)S(1)} %fusion.47, s32[]{:T(128)} %constant.166.clone.1), window={size=1x1x128 pad=0_0x0_0x127_0}, to_apply=%region_0.1 | reduce-window | flops 4161536 | bytes 262148 | tf_op jit(solution)/shard_map/reduce-window
  15.8 14.6 %scatter_custom_fusion = bf16[1536]{0:T(1024)(128)(2,1)S(1)} fusion(s32[2048]{0:T(1024)S(1)} %bitcast.199, bf16[2048]{0:T(1024)(128)(2,1)S(1)} %reshape.395, bf16[]{:T(256)} %constant.174.clone.1), kind=kCustom, calls=%fused_computation.118 | custom fusion | bytes 3074 | tf_op jit(solution)/shard_map/scatter | solution.py:176
  31.0 5.2 %all-to-all-start = ((bf16[8,1,192]{2,1,0:T(2,128)(2,1)}), bf16[8,1,192]{2,1,0:T(2,128)(2,1)S(1)}, u32[]{:S(2)}, u32[]{:S(2)}) async-start(bf16[8,1,192]{2,1,0:T(2,128)(2,1)} %all_to_all.16), calls=%async_computation | async-start | bytes 16384 | tf_op jit(solution)/shard_map/all_to_all | solution.py:185
  36.2 8.0 %scatter_custom_fusion.1 = s32[1536]{0:T(1024)S(1)} fusion(s32[2048]{0:T(1024)S(1)} %bitcast.200, s32[2048]{0:T(1024)S(1)} %add_select_fusion.2, s32[]{:T(128)} %constant.175.clone.1), kind=kCustom, calls=%fused_computation.116 | custom fusion | bytes 6148 | tf_op jit(solution)/shard_map/scatter | solution.py:172
  44.4 1.3 concatenate.3
  45.7 7.1 %gather_fusion = bf16[1536,2048]{1,0:T(8,128)(2,1)} fusion(bf16[257,2048]{1,0:T(8,128)(2,1)S(1)} %concatenate.3, s32[2048]{0:T(1024)S(1)} %pad_clamp_fusion), kind=kCustom, calls=%fused_computation | custom fusion | bytes 12589056 | tf_op jit(solution)/shard_map/jit(_take)/gather | solution.py:179
  52.9 6.1 %broadcast_select_fusion = bf16[8,192,2048]{2,1,0:T(8,128)(2,1)} fusion(bf16[8,192,2048]{2,1,0:T(8,128)(2,1)} %bitcast.173, pred[8,192]{1,0:T(8,128)(4,1)S(1)} %broadcast_in_dim.109), kind=kLoop, calls=%fused_computation.10 | loop fusion | flops 3145728 | bytes 12584448 | tf_op jit(solution)/shard_map/jit(_take)/select_n | solution.py:179
  59.0 4.9 %all-to-all-start.1 = ((bf16[8,192,2048]{2,1,0:T(8,128)(2,1)}), bf16[8,192,2048]{2,1,0:T(8,128)(2,1)}, u32[]{:S(2)}, u32[]{:S(2)}) async-start(bf16[8,192,2048]{2,1,0:T(8,128)(2,1)} %broadcast_select_fusion), calls=%async_computation.1 | async-start | bytes 12582912 | tf_op jit(solution)/shard_map/all_to_all | solution.py:184
  63.9 71.5 %all-to-all-done.1 = bf16[8,192,2048]{2,1,0:T(8,128)(2,1)} async-done(((bf16[8,192,2048]{2,1,0:T(8,128)(2,1)}), bf16[8,192,2048]{2,1,0:T(8,128)(2,1)}, u32[]{:S(2)}, u32[]{:S(2)}) %all-to-all-start.1) | async-done | bytes 6291488 | tf_op jit(solution)/shard_map/all_to_all | solution.py:184
  135.5 4.0 %multiply_convert_fusion = bf16[8,192,2048]{2,1,0:T(8,128)(2,1)S(1)} fusion(bf16[8,192,2048]{2,1,0:T(8,128)(2,1)} %all-to-all-done.1, f32[8,192]{1,0:T(8,128)S(1)} %bitcast.198), kind=kLoop, calls=%fused_computation.8 | loop fusion | flops 9437184 | bytes 12589056 | tf_op jit(solution)/shard_map/convert_element_type | solution.py:187
  139.8 4.9 %fusion.11 = (bf16[1536,512]{1,0:T(8,128)(2,1)S(1)}, bf16[1536,512]{1,0:T(8,128)(2,1)S(1)}) fusion(bf16[1,8,192,512]{3,2,1,0:T(8,128)(2,1)S(1)} %copy-done.6, bf16[1,8,192,512]{3,2,1,0:T(8,128)(2,1)S(1)} %copy-done.7, bf16[1536,2048]{1,0:T(8,128)(2,1)S(1)} %bitcast.175, bf16[1,512,2048]{2,1,0:T(8,128)(2,1)S(1)} %copy-done.13), kind=kOutput, calls=%fused_computation.28 | convolution fusion | flops 3233021952 | bytes 14680064 | tf_op jit(solution)/shard_map/dot_general | solution.py:45
  144.7 6.5 %fusion.15 = f32[1536,2048]{1,0:T(8,128)} fusion(bf16[1536,512]{1,0:T(8,128)(2,1)S(1)} %get-tuple-element.267, bf16[1,2048,512]{2,1,0:T(8,128)(2,1)S(1)} %copy-done), kind=kOutput, calls=%fused_computation.33 | convolution fusion | flops 3221225472 | bytes 16252928 | tf_op jit(solution)/shard_map/dot_general | solution.py:59
  151.2 8.3 %add_convert_fusion = bf16[1536,2048]{1,0:T(8,128)(2,1)} fusion(f32[1536,2048]{1,0:T(8,128)} %fusion.15, bf16[1536,512]{1,0:T(8,128)(2,1)S(1)} %get-tuple-element.266, bf16[1,2048,512]{2,1,0:T(8,128)(2,1)S(1)} %copy-done.14), kind=kOutput, calls=%fused_computation.7 | convolution fusion | flops 3227516928 | bytes 22544384 | tf_op jit(solution)/shard_map/dot_general | solution.py:62
  159.6 4.8 %all-to-all-start.2 = ((bf16[8,192,2048]{2,1,0:T(8,128)(2,1)}), bf16[8,192,2048]{2,1,0:T(8,128)(2,1)}, u32[]{:S(2)}, u32[]{:S(2)}) async-start(bf16[8,192,2048]{2,1,0:T(8,128)(2,1)} %bitcast.174), calls=%async_computation.2 | async-start | bytes 12582912 | tf_op jit(solution)/shard_map/all_to_all | solution.py:193
  164.9 71.0 %all-to-all-done.2 = bf16[8,192,2048]{2,1,0:T(8,128)(2,1)} async-done(((bf16[8,192,2048]{2,1,0:T(8,128)(2,1)}), bf16[8,192,2048]{2,1,0:T(8,128)(2,1)}, u32[]{:S(2)}, u32[]{:S(2)}) %all-to-all-start.2) | async-done | bytes 6291488 | tf_op jit(solution)/shard_map/all_to_all | solution.py:193
  235.9 20.0 %gather_fusion.1 = bf16[2048,2048]{1,0:T(8,128)(2,1)} fusion(bf16[1536,2048]{1,0:T(8,128)(2,1)} %bitcast.21, s32[2048]{0:T(1024)S(1)} %broadcast_clamp_fusion), kind=kCustom, calls=%fused_computation.1 | custom fusion | bytes 16785408 | tf_op jit(solution)/shard_map/jit(_take)/gather | solution.py:73
  255.9 10.6 %multiply_reduce_fusion = f32[256,2048]{1,0:T(8,128)} fusion(bf16[2048,2048]{1,0:T(8,128)(2,1)} %gather_fusion.1, f32[256,8]{1,0:T(8,128)S(1)} %convert_element_type.196, pred[256,8]{1,0:T(8,128)(4,1)S(1)} %get-tuple-element.261), kind=kLoop, calls=%fused_computation.6 | loop fusion | flops 16252928 | bytes 10496000 | tf_op jit(solution)/shard_map/reduce_sum | solution.py:75
  267.3 1.3 broadcast_compare_fusion
  272.9 1.4 dynamic-update-slice.2
  274.3 1.4 dynamic-update-slice.3
  276.4 12.7 %all-reduce.5 = (bf16[8]{0:T(256)(128)(2,1)S(1)}, bf16[8]{0:T(256)(128)(2,1)S(1)}, bf16[8]{0:T(256)(128)(2,1)S(1)}, bf16[8]{0:T(256)(128)(2,1)S(1)}) all-reduce(bf16[8]{0:T(256)(128)(2,1)S(1)} %dynamic-update-slice, bf16[8]{0:T(256)(128)(2,1)S(1)} %dynamic-update-slice.1, ...), channel_id=1, replica_groups=mesh['ctx'=8,'ep'=4] {'ctx'}, use_global_device_ids=true, to_apply=%add.1 | all-reduce | flops 32 | bytes 128
  289.8 4.1 %fusion.13 = bf16[1,8,192,512]{3,2,1,0:T(8,128)(2,1)} fusion(bf16[1,8,192,512]{3,2,1,0:T(8,128)(2,1)} %param.20, bf16[1,8,192,512]{3,2,1,0:T(8,128)(2,1)} %param.21), kind=kLoop, calls=%fused_computation.31 | loop fusion | flops 6291456 | bytes 4718592 | tf_op jit(solution)/shard_map/convert_element_type | solution.py:51
  293.8 15.9 %reduce-scatter.2.cloned.1.call-done = f32[256,512]{1,0:T(8,128)} async-done(((f32[256,2048]{1,0:T(8,128)}), f32[256,512]{1,0:T(8,128)}) %reduce-scatter.2.cloned.1.call-update) | async-done | bytes 524304 | tf_op jit(solution)/shard_map/reduce_scatter | solution.py:204
  312.0 8.8 %convolution_bitcast_fusion = f32[1,512,2048]{2,1,0:T(8,128)} fusion(bf16[1536,512]{1,0:T(8,128)(2,1)} %bitcast.188, bf16[1536,2048]{1,0:T(8,128)(2,1)} %bitcast.176), kind=kOutput, calls=%fused_computation.11 | convolution fusion | flops 3221225472 | bytes 12058624 | tf_op jit(solution)/shard_map/dot_general | solution.py:52
  321.1 13.4 %all-gather.7.cloned.1.call-done = bf16[32,128,128]{2,1,0:T(8,128)(2,1)} async-done(((bf16[4,128,128]{2,1,0:T(8,128)(2,1)}), bf16[32,128,128]{2,1,0:T(8,128)(2,1)}) %all-gather.7.cloned.1.call-update) | async-done | bytes 1048592 | tf_op jit(solution)/shard_map/all_gather | solution.py:17
  334.5 37.2 %while.33 = (s32[]{:T(128)}, f32[4,128,128]{2,1,0:T(8,128)S(1)}, f32[]{:T(128)}, s32[]{:T(128)}, bf16[8,4,128,128]{3,2,1,0:T(8,128)(2,1)}, /*index=5*/bf16[8]{0:...) while((s32[]{:T(128)}, f32[4,128,128]{2,1,0:T(8,128)S(1)}, ...), condition=%wide.region_10.11_spmd, body=%wide.region_9.10_spmd.sunk | while | flops 196620 | bytes 655598 | solution.py:34
  373.4 1.2 fusion.25
  374.6 1.9 copy.108
  376.5 2.3 fusion.24
  378.9 1.8 copy.107
  380.7 1.3 fusion.22
  382.0 1.7 fusion.23
  (118 shorter events, 34.2 us)
Async XLA Ops:
  8.0 136.7 %copy-start = (bf16[1,2048,512]{2,1,0:T(8,128)(2,1)S(1)}, bf16[1,2048,512]{2,1,0:T(8,128)(2,1)}, u32[]{:S(2)}) copy-start(bf16[1,2048,512]{2,1,0:T(8,128)(2,1)} %param.22) | copy-start | bytes 6291460
  31.0 27.9 %all-to-all-start = ((bf16[8,1,192]{2,1,0:T(2,128)(2,1)}), bf16[8,1,192]{2,1,0:T(2,128)(2,1)S(1)}, u32[]{:S(2)}, u32[]{:S(2)}) async-start(bf16[8,1,192]{2,1,0:T(2,128)(2,1)} %all_to_all.16), calls=%async_computation | async-start | bytes 16384 | tf_op jit(solution)/shard_map/all_to_all | solution.py:185
  59.0 76.5 %all-to-all-start.1 = ((bf16[8,192,2048]{2,1,0:T(8,128)(2,1)}), bf16[8,192,2048]{2,1,0:T(8,128)(2,1)}, u32[]{:S(2)}, u32[]{:S(2)}) async-start(bf16[8,192,2048]{2,1,0:T(8,128)(2,1)} %broadcast_select_fusion), calls=%async_computation.1 | async-start | bytes 12582912 | tf_op jit(solution)/shard_map/all_to_all | solution.py:184
  135.4 4.0 %copy-start.6 = (bf16[1,8,192,512]{3,2,1,0:T(8,128)(2,1)S(1)}, bf16[1,8,192,512]{3,2,1,0:T(8,128)(2,1)}, u32[]{:S(2)}) copy-start(bf16[1,8,192,512]{3,2,1,0:T(8,128)(2,1)} %param.20) | copy-start | bytes 4718596
  135.4 4.0 %copy-start.7 = (bf16[1,8,192,512]{3,2,1,0:T(8,128)(2,1)S(1)}, bf16[1,8,192,512]{3,2,1,0:T(8,128)(2,1)}, u32[]{:S(2)}) copy-start(bf16[1,8,192,512]{3,2,1,0:T(8,128)(2,1)} %param.21) | copy-start | bytes 4718596
  135.5 4.4 %copy-start.13 = (bf16[1,512,2048]{2,1,0:T(8,128)(2,1)S(1)}, bf16[1,512,2048]{2,1,0:T(8,128)(2,1)}, u32[]{:S(2)}) copy-start(bf16[1,512,2048]{2,1,0:T(8,128)(2,1)} %param.24) | copy-start | bytes 6291460
  139.5 5.2 %copy-start.2 = (bf16[8,192,2048]{2,1,0:T(8,128)(2,1)}, bf16[8,192,2048]{2,1,0:T(8,128)(2,1)S(1)}, u32[]{:S(2)}) copy-start(bf16[8,192,2048]{2,1,0:T(8,128)(2,1)S(1)} %multiply_convert_fusion) | copy-start | bytes 18874372
  144.7 6.5 %copy-start.14 = (bf16[1,2048,512]{2,1,0:T(8,128)(2,1)S(1)}, bf16[1,2048,512]{2,1,0:T(8,128)(2,1)}, u32[]{:S(2)}) copy-start(bf16[1,2048,512]{2,1,0:T(8,128)(2,1)} %param.23) | copy-start | bytes 6291460
  159.6 76.3 %all-to-all-start.2 = ((bf16[8,192,2048]{2,1,0:T(8,128)(2,1)}), bf16[8,192,2048]{2,1,0:T(8,128)(2,1)}, u32[]{:S(2)}, u32[]{:S(2)}) async-start(bf16[8,192,2048]{2,1,0:T(8,128)(2,1)} %bitcast.174), calls=%async_computation.2 | async-start | bytes 12582912 | tf_op jit(solution)/shard_map/all_to_all | solution.py:193
  164.3 145.4 %reduce-scatter.2.cloned.1.call-start = ((), (), s32[]{:S(2)}) async-start(), calls=%async_computation.4 | async-start | bytes 2621440 | tf_op jit(solution)/shard_map/reduce_scatter | solution.py:204
  255.9 10.7 %copy-start.10 = (bf16[256,512]{1,0:T(8,128)(2,1)S(1)}, bf16[256,512]{1,0:T(8,128)(2,1)}, u32[]{:S(2)}) copy-start(bf16[256,512]{1,0:T(8,128)(2,1)} %param.26) | copy-start | bytes 786436
  255.9 10.9 %copy-start.12 = (s32[256]{0:T(256)S(1)}, s32[256]{0:T(256)}, u32[]{:S(2)}) copy-start(s32[256]{0:T(256)} %param.19) | copy-start | bytes 3076
  255.9 12.8 %copy-start.8 = (bf16[256,512]{1,0:T(8,128)(2,1)S(1)}, bf16[256,512]{1,0:T(8,128)(2,1)}, u32[]{:S(2)}) copy-start(bf16[256,512]{1,0:T(8,128)(2,1)} %param.27) | copy-start | bytes 786436
  266.5 4.4 %copy-start.15 = (u32[32]{0:T(128)S(1)}, u32[32]{0:T(128)}, u32[]{:S(2)}) copy-start(u32[32]{0:T(128)} %constant.195) | copy-start | bytes 388
  266.5 22.6 %copy-start.11 = (bf16[256,512]{1,0:T(8,128)(2,1)S(1)}, bf16[256,512]{1,0:T(8,128)(2,1)}, u32[]{:S(2)}) copy-start(bf16[256,512]{1,0:T(8,128)(2,1)} %param.25) | copy-start | bytes 786436
  266.5 45.4 %all-gather.5.cloned.1.call-start = ((), (), s32[]{:S(2)}) async-start(), calls=%async_computation.5 | async-start | bytes 1179648 | tf_op jit(solution)/shard_map/all_gather | solution.py:17
  266.7 105.0 %copy-start.3 = (bf16[256,512]{0,1:T(8,128)(2,1)}, bf16[256,512]{0,1:T(8,128)(2,1)S(1)}, u32[]{:S(2)}) copy-start(bf16[256,512]{0,1:T(8,128)(2,1)S(1)} %copy.112) | copy-start | bytes 786436
  269.5 64.9 %all-gather.7.cloned.1.call-start = ((), (), s32[]{:S(2)}) async-start(), calls=%async_computation.6 | async-start | bytes 1179648 | tf_op jit(solution)/shard_map/all_gather | solution.py:17
  289.3 21.7 %copy-start.5 = (bf16[256,512]{0,1:T(8,128)(2,1)}, bf16[256,512]{0,1:T(8,128)(2,1)S(1)}, u32[]{:S(2)}) copy-start(bf16[256,512]{0,1:T(8,128)(2,1)S(1)} %copy.113) | copy-start | bytes 786436
  310.9 62.4 %copy-start.4 = (bf16[256,512]{0,1:T(8,128)(2,1)}, bf16[256,512]{0,1:T(8,128)(2,1)S(1)}, u32[]{:S(2)}) copy-start(bf16[256,512]{0,1:T(8,128)(2,1)S(1)} %copy.111) | copy-start | bytes 786436
  312.0 8.8 %copy-start.9 = (bf16[256,512]{1,0:T(8,128)(2,1)S(1)}, bf16[256,512]{1,0:T(8,128)(2,1)}, u32[]{:S(2)}) copy-start(bf16[256,512]{1,0:T(8,128)(2,1)} %param.27) | copy-start | bytes 786436
  374.6 9.9 %copy-start.1 = (bf16[1,2048,512]{2,1,0:T(8,128)(2,1)S(1)}, bf16[1,2048,512]{2,1,0:T(8,128)(2,1)}, u32[]{:S(2)}) copy-start(bf16[1,2048,512]{2,1,0:T(8,128)(2,1)} %param.22) | copy-start | bytes 6291460
Sparse Core Ops, SparseCore 0:
  266.6 43.0 reduce-scatter.1
Sparse Core Ops, SparseCore 1:
  269.6 22.7 all-gather.4
  312.0 22.4 all-gather.6
where the time goes:
time: 393 us; the launch traced here: 392 us
  waiting for transfers between devices  172 us (44%)
  local copies, waits for them, and re-layouts  78.5 us (20%)
  other arithmetic  39.4 us (10%)
  matrix products  39.1 us (10%)
  loops' own time  18 us (5%)
  between operations  17.3 us (4%)
  starting transfers between devices  15.3 us (4%)
  blocking collectives  12.7 us (3%)
    all_to_all x1, waiting for transfers between devices, local(): lax.all_to_all(send_rows, 'ctx', split_axis=0, concat_axis=0, tiled=True)  71.5 us
    all_to_all x1, waiting for transfers between devices, local(): lax.all_to_all(input_part.reshape(owners, slot_count, model_width), 'ctx'...  71 us
    gather x1, local copies, waits for them, and re-layouts, gather_back(): jnp.take(returned.reshape(-1, model_width), row_index, axis=0)  20 us
    another operation x2, loops' own time, prefix(): return lax.fori_loop(0, ahead, one, state)  18 us
    reduce_scatter x1, waiting for transfers between devices, local(): lax.psum_scatter(token_sum, 'ep', scatter_dimension=1, tiled=True)  15.9 us
    scatter x1, local copies, waits for them, and re-layouts, local(): slot_gate = jnp.zeros((dump_slot,), gate_values.dtype).at[position].set(g...  14.6 us
    all_gather x2, waiting for transfers between devices, prefix(): lax.all_gather(a.astype(kind), axis)  13.4 us
    unnamed x1, blocking collectives  12.7 us
  transfers between devices with their start and end apart: 6, of which 4 were waited for; matrix products, arithmetic and copies ran while one was open for 12% of the time, Pallas kernels for 0%

commit v1 on v0

v1 whole, which is shorter than its diff:
```python
import functools

import jax
import jax.numpy as jnp
from jax import lax
from jax.experimental import pallas as pl
from jax.experimental.pallas import tpu as pltpu
from jax.sharding import PartitionSpec as P


HEAD_DIM = 128
BF16 = jnp.bfloat16
F32 = jnp.float32


def dot(a, b, dims):
    return lax.dot_general(a, b, ((dims[:1], dims[1:]), ((), ())), preferred_element_type=F32)


def swap(x, axis, offset):
    return lax.ppermute(x, axis, [(i, i ^ offset) for i in range(lax.axis_size(axis))])


def after(x, *others):
    return lax.optimization_barrier((x, *others))[0]


def expert_kernel(scal, *refs, count, groups, tok, slots):
    routes, refs = refs[:count], refs[count:]
    early, refs = refs[:count], refs[count:]
    late, refs = refs[:count], refs[count:]
    pres, refs = refs[:count], refs[count:]
    ups, refs = refs[:count], refs[count:]
    w_down, w_gate, w_up = refs[:3]
    lows, highs = refs[3 : 3 + count], refs[3 + count : 3 + 2 * count]
    cot, hidden, token, pick, back, part, gate_delta, up_delta = refs[3 + 2 * count :]
    step = pl.program_id(0)

    @pl.when(step == 0)
    def _():
        token[...] = jnp.zeros_like(token)
        expert = scal[0].astype(F32)
        t_row = lax.broadcasted_iota(jnp.int32, (tok, tok), 0)
        t_col = lax.broadcasted_iota(jnp.int32, (tok, tok), 1)
        earlier = (t_row < t_col).astype(F32).astype(BF16)
        slot = lax.broadcasted_iota(jnp.int32, (slots, tok), 0)
        for i, route in enumerate(routes):
            gates = route[:, :tok].astype(F32)
            named = route[:, tok : 2 * tok].astype(F32) == expert
            gate = jnp.sum(jnp.where(named, gates, 0.0), axis=0, keepdims=True)
            mine = jnp.sum(named.astype(F32), axis=0, keepdims=True)
            spread = jnp.broadcast_to(mine, (8, tok)).astype(BF16)
            rank = dot(spread, earlier, (1, 0))[:1].astype(jnp.int32)
            chosen = jnp.where((slot == rank) & (mine > 0.0), 1.0, 0.0)
            pick[i] = (chosen * gate).astype(BF16)
            back[i] = chosen.T.astype(BF16)

    def gather(rows):
        for i in range(count):
            cot[i * slots : (i + 1) * slots, :] = dot(pick[i], rows[i][...], (1, 0)).astype(BF16)
        return dot(cot[...], w_down[...], (1, 1))

    @pl.when(step == 0)
    def _():
        part[...] = gather(early)

    @pl.when(step == 1)
    def _():
        part[...] += gather(late)
        for i in range(count):
            here = pl.ds(i * slots, slots)
            a = pres[i][0].astype(F32)
            u = ups[i][0].astype(F32)
            s = jax.nn.sigmoid(a)
            d = part[here, :]
            hidden[here, :] = (a * s * u).astype(BF16)
            gate_delta[here, :] = (d * u * s * (1.0 + a * (1.0 - s))).astype(BF16)
            up_delta[here, :] = (d * a * s).astype(BF16)

    @pl.when(step >= 2)
    def _():
        both = dot(gate_delta[...], w_gate[...], (1, 1)) + dot(up_delta[...], w_up[...], (1, 1))
        both = both.astype(BF16)
        half = both.shape[1] // groups
        for i in range(count):
            y = dot(back[i], both[i * slots : (i + 1) * slots], (1, 0)).astype(BF16)
            for g in range(groups // 2):
                there = pl.ds(g * half, half)
                lows[i][:, there] = y[:, 2 * g * half : (2 * g + 1) * half]
                highs[i][:, there] = y[:, (2 * g + 1) * half : (2 * g + 2) * half]


def expert_group(scal, loads, gate_pre, up_pre, w_gate, w_up, w_down, groups):
    _, slots, ffp = gate_pre.shape
    count = len(loads)
    tok = loads[0][0].shape[0] - 8
    width = w_gate.shape[0]
    chunk = width // 2

    def early(i):
        return jnp.minimum(i, 1)

    def late(i):
        return jnp.maximum(i - 2, 0)

    route = pl.BlockSpec((8, 4 * tok), lambda i, s: (tok // 8, 0))
    first = pl.BlockSpec((tok, chunk), lambda i, s: (0, 0))
    seconds = [
        pl.BlockSpec((tok, chunk), functools.partial(lambda i, s, skip: (0, skip), skip=b.shape[1] // chunk - 1))
        for a, b in loads
    ]
    pres = [
        pl.BlockSpec((1, slots, ffp), functools.partial(lambda i, s, n: (s[1 + n], 0, 0), n=n))
        for n in range(count)
    ]
    down = pl.BlockSpec((ffp, chunk), lambda i, s: (0, s[1 + count + early(i)]))
    up = pl.BlockSpec((chunk, ffp), lambda i, s: (late(i), 0))
    y = pl.BlockSpec((tok, chunk // 2), lambda i, s: (0, late(i)))
    half_rows = jax.ShapeDtypeStruct((tok, width // 2), BF16)
    m = count * slots
    outs = pl.pallas_call(
        functools.partial(expert_kernel, count=count, groups=groups, tok=tok, slots=slots),
        grid_spec=pltpu.PrefetchScalarGridSpec(
            num_scalar_prefetch=1,
            grid=(4,),
            in_specs=[route] * count + [first] * count + seconds + pres * 2 + [down, up, up],
            out_specs=[y] * (2 * count)
            + [
                pl.BlockSpec((m, chunk), lambda i, s: (0, s[1 + count + early(i)])),
                pl.BlockSpec((m, ffp), lambda i, s: (0, 0)),
                pl.BlockSpec((8, 128), lambda i, s: (0, 0)),
            ],
            scratch_shapes=[
                pltpu.VMEM((count, slots, tok), BF16),
                pltpu.VMEM((count, tok, slots), BF16),
                pltpu.VMEM((m, ffp), F32),
                pltpu.VMEM((m, ffp), BF16),
                pltpu.VMEM((m, ffp), BF16),
            ],
        ),
        out_shape=[half_rows] * (2 * count)
        + [
            jax.ShapeDtypeStruct((m, width), BF16),
            jax.ShapeDtypeStruct((m, ffp), BF16),
            jax.ShapeDtypeStruct((8, 128), F32),
        ],
        cost_estimate=pl.CostEstimate(
            flops=4 * m * width * (3 * ffp + 2 * tok), transcendentals=m * ffp, bytes_accessed=4 * m * width
        ),
        name="expert_group",
    )(
        scal,
        *[a for a, b in loads],
        *[a for a, b in loads],
        *[b for a, b in loads],
        *[gate_pre] * count,
        *[up_pre] * count,
        w_down,
        w_gate,
        w_up,
    )
    return outs[:count], outs[count : 2 * count], *outs[-3:]


def small_cost(us):
    return pl.CostEstimate(flops=int(us * 7e8), transcendentals=0, bytes_accessed=1 << 16)


def head_of(ref, h):
    return ref[:, h * HEAD_DIM : (h + 1) * HEAD_DIM]


def state_kernel(seg, left, right, out, *, edge, heads):
    keep = seg[...] == seg[edge : edge + 1, :]
    rows = jnp.where(keep, left[...].astype(F32), 0.0).astype(BF16)
    for h in range(heads):
        out[h] = dot(head_of(rows, h), head_of(right, h), (0, 0)).astype(BF16)


def columns(x, part, parts):
    return pl.BlockSpec((x.shape[0], x.shape[1] // parts), lambda i: (0, part))


def edge_state(seg_col, left, right, edge, part, parts):
    wide = left.shape[1] // parts
    heads = wide // HEAD_DIM
    whole = pl.BlockSpec((heads, HEAD_DIM, HEAD_DIM), lambda i: (0, 0, 0))
    right_parts = right.shape[1] // wide
    return pl.pallas_call(
        functools.partial(state_kernel, edge=edge, heads=heads),
        grid=(1,),
        in_specs=[columns(seg_col, 0, 1), columns(left, part, parts), columns(right, part % right_parts, right_parts)],
        out_specs=whole,
        out_shape=jax.ShapeDtypeStruct((heads, HEAD_DIM, HEAD_DIM), BF16),
        cost_estimate=small_cost(1),
        name="edge_state",
    )(seg_col, left, right)


def weighted(weights, side, states, shards):
    total = None
    for r in range(1, shards):
        w = weights[side : side + 1, r : r + 1]
        add = jnp.where(w[None] > 0.0, states[r][...].astype(F32), 0.0)
        total = add if total is None else total + add
    return total.astype(BF16)


def inner_kernel(weights, seg_col, seg_row, q, k, v, g, *refs, shards, tok, heads):
    states = (None, *refs[: shards - 1])
    dq, dk, dv = refs[-3:]
    col = seg_col[...]
    t_row = lax.broadcasted_iota(jnp.int32, (tok, tok), 0)
    t_col = lax.broadcasted_iota(jnp.int32, (tok, tok), 1)
    allowed = (t_row >= t_col) & (col == seg_row[...])
    before = col == col[:1, :]
    fwd = weighted(weights, 0, states, shards)
    for h in range(heads):
        qh, kh, vh, gh = head_of(q, h), head_of(k, h), head_of(v, h), head_of(g, h)
        here = pl.ds(h * HEAD_DIM, HEAD_DIM)
        cot_value = jnp.where(allowed, dot(gh, vh, (1, 1)), 0.0).astype(BF16)
        query_key = jnp.where(allowed, dot(qh, kh, (1, 1)), 0.0).astype(BF16)
        outer = jnp.where(before, dot(gh, fwd[h], (1, 1)), 0.0)
        dq[:, here] = (dot(cot_value, kh, (1, 0)) + outer).astype(BF16)
        dk[:, here] = dot(cot_value, qh, (0, 0))
        dv[:, here] = dot(query_key, gh, (0, 0))


def outer_kernel(weights, seg_col, k, v, dk_in, dv_in, *refs, shards, tok, heads):
    states = (None, *refs[: shards - 1])
    dk, dv = refs[-2:]
    col = seg_col[...]
    follow = col == col[tok - 1 :, :]
    back = weighted(weights, 1, states, shards)
    for h in range(heads):
        here = pl.ds(h * HEAD_DIM, HEAD_DIM)
        k_outer = jnp.where(follow, dot(head_of(v, h), back[h], (1, 1)), 0.0)
        v_outer = jnp.where(follow, dot(head_of(k, h), back[h], (1, 0)), 0.0)
        dk[:, here] = (dk_in[:, here] + k_outer).astype(BF16)
        dv[:, here] = (dv_in[:, here] + v_outer).astype(BF16)


def inner_grads(weights, seg_col, seg_row, q, k, v, g, states, part, parts, dq):
    tok, width = q.shape
    wide = width // parts
    heads = wide // HEAD_DIM
    shards = len(states) + 1
    mine = pl.BlockSpec((tok, wide), lambda i: (0, part))
    own = pl.BlockSpec((tok, wide), lambda i: (0, 0))
    state = pl.BlockSpec((heads, HEAD_DIM, HEAD_DIM), lambda i: (part, 0, 0))
    filled = [] if dq is None else [dq]
    return pl.pallas_call(
        functools.partial(inner_kernel, shards=shards, tok=tok, heads=heads),
        grid=(1,),
        in_specs=[
            pl.BlockSpec((8, 128), lambda i: (0, 0)),
            columns(seg_col, 0, 1),
            columns(seg_row, 0, 1),
            mine, mine, mine, own,
            *[state] * (shards - 1),
            *[pl.BlockSpec(memory_space=pl.ANY) for _ in filled],
        ],
        out_specs=[mine, own, own],
        out_shape=[
            jax.ShapeDtypeStruct((tok, width), BF16),
            jax.ShapeDtypeStruct((tok, wide), F32),
            jax.ShapeDtypeStruct((tok, wide), F32),
        ],
        input_output_aliases={6 + shards: 0} if filled else {},
        cost_estimate=small_cost(3),
        name="inner_grads",
    )(weights, seg_col, seg_row, q, k, v, g, *states, *filled)


def outer_grads(weights, seg_col, k, v, dk, dv, states, part, parts, filled):
    tok, width = k.shape
    wide = width // parts
    heads = wide // HEAD_DIM
    shards = len(states) + 1
    mine = pl.BlockSpec((tok, wide), lambda i: (0, part))
    own = pl.BlockSpec((tok, wide), lambda i: (0, 0))
    state = pl.BlockSpec((heads, HEAD_DIM, HEAD_DIM), lambda i: (0, 0, 0))
    return pl.pallas_call(
        functools.partial(outer_kernel, shards=shards, tok=tok, heads=heads),
        grid=(1,),
        in_specs=[
            pl.BlockSpec((8, 128), lambda i: (0, 0)),
            columns(seg_col, 0, 1),
            mine, mine, own, own,
            *[state] * (shards - 1),
            *[pl.BlockSpec(memory_space=pl.ANY) for _ in filled],
        ],
        out_specs=[mine, mine],
        out_shape=[jax.ShapeDtypeStruct((tok, width), BF16)] * 2,
        input_output_aliases={5 + shards: 0, 6 + shards: 1} if filled else {},
        cost_estimate=small_cost(2),
        name="outer_grads",
    )(weights, seg_col, k, v, dk, dv, *states, *filled)


def load_kernel(scal, rows, gates, ids, seg, load, half, seg_col, *, tok, width):
    start = pl.multiple_of(scal[0] * (width // 2), width // 2)
    load[:tok, :] = rows[...]
    half[:tok, :] = rows[:, pl.ds(start, width // 2)]
    gate_rows = gates[...].astype(F32)
    id_rows = ids[...].astype(F32)
    seg_rows = jnp.broadcast_to(seg[...].astype(F32), (128, tok))
    seg_col[...] = seg_rows.T[:, :1]
    rest = jnp.zeros((8, width // 2 - 3 * tok), F32)
    route = jnp.concatenate([gate_rows, id_rows, seg_rows[:8], rest], axis=1).astype(BF16)
    load[tok:, : width // 2] = route
    load[tok:, width // 2 :] = route
    half[tok:, :] = route


def make_load(parity, rows, gates, ids, seg):
    tok, width = rows.shape

    def whole(shape):
        return pl.BlockSpec(shape, lambda i, s: (0, 0))

    shapes = [(tok + 8, width), (tok + 8, width // 2), (tok, 1)]
    return pl.pallas_call(
        functools.partial(load_kernel, tok=tok, width=width),
        grid_spec=pltpu.PrefetchScalarGridSpec(
            num_scalar_prefetch=1,
            grid=(1,),
            in_specs=[whole(x.shape) for x in (rows, gates, ids, seg)],
            out_specs=[whole(x) for x in shapes],
        ),
        out_shape=[jax.ShapeDtypeStruct(x, t) for x, t in zip(shapes, (BF16, BF16, F32))],
        cost_estimate=small_cost(2),
        name="make_load",
    )(parity[None], rows, gates, ids, seg)


def weight_kernel(scal, *refs, shards, tok):
    routes, out = refs[:shards], refs[shards]
    me = scal[0]
    first = routes[0][:1, 2 * tok : 2 * tok + 1].astype(F32)
    last = routes[0][:1, 3 * tok - 1 : 3 * tok].astype(F32)
    side = lax.broadcasted_iota(jnp.int32, (8, 128), 0)
    lane = lax.broadcasted_iota(jnp.int32, (8, 128), 1)
    total = jnp.zeros((8, 128), F32)
    for r in range(1, shards):
        other = me ^ r
        first_r = routes[r][:1, 2 * tok : 2 * tok + 1].astype(F32)
        last_r = routes[r][:1, 3 * tok - 1 : 3 * tok].astype(F32)
        earlier = (last_r == first) & (other < me) & (side == 0)
        later = (first_r == last) & (other > me) & (side == 1)
        total = jnp.where((lane == r) & (earlier | later), 1.0, total)
    out[...] = total


def state_weights(me, loads, tok):
    shards = len(loads)
    return pl.pallas_call(
        functools.partial(weight_kernel, shards=shards, tok=tok),
        grid_spec=pltpu.PrefetchScalarGridSpec(
            num_scalar_prefetch=1,
            grid=(1,),
            in_specs=[pl.BlockSpec((8, 4 * tok), lambda i, s: (tok // 8, 0))] * shards,
            out_specs=pl.BlockSpec((8, 128), lambda i, s: (0, 0)),
        ),
        out_shape=jax.ShapeDtypeStruct((8, 128), F32),
        cost_estimate=small_cost(1),
        name="state_weights",
    )(me[None], *loads)


def all_states(own, chips):
    near = [own] + [swap(own, "ctx", 2 * j) for j in range(1, chips)]
    far = [swap(x, "ctx", 1) for x in near]
    return [(near if r % 2 == 0 else far)[r // 2] for r in range(1, 2 * chips)]


def local(
    out_grad, gate_values, expert_ids, segment_ids, gate_pre, up_pre, w_gate, w_up, w_down,
    queries, keys, values,
):
    shards = lax.axis_size("ctx")
    groups = lax.axis_size("ep")
    chips = shards // 2
    me = lax.axis_index("ctx").astype(jnp.int32)
    place = lax.axis_index("ep").astype(jnp.int32)
    parity = place % 2
    tok, width = out_grad.shape
    expert = 2 * me + place // (groups // 2)
    corners = [3] if chips == 4 else []
    sides = [j for j in range(1, chips) if j not in corners]
    weights3 = (w_gate[0], w_up[0], w_down[0])

    seg_row = segment_ids[None, :]
    load, mine, seg_col = make_load(parity, out_grad, gate_values.T, expert_ids.T, seg_row)
    seg_row = seg_row.astype(F32)
    near = {0: (load, load)}
    far = {}
    corner_half = {j: swap(mine, "ctx", 2 * j) for j in corners}
    far[0] = (swap(load, "ctx", 1),) * 2
    for j in sides:
        near[j] = (swap(load, "ctx", 2 * j),) * 2

    straight = [jnp.int32(0), jnp.int32(1)]
    turned = [parity, 1 - parity]

    def experts(js, order, token):
        loads, sources = [], []
        for j in js:
            loads += [near[j], far[j]]
            sources += [me ^ (2 * j), me ^ (2 * j + 1)]
        scal = jnp.stack([expert, *sources, *order])
        if token is not None:
            scal = after(scal, *token)
        low, high, cot, hidden, token = expert_group(
            scal, loads, gate_pre[0], up_pre[0], *weights3, groups
        )
        cots.append(cot)
        hiddens.append(hidden)
        for i, j in enumerate(js):
            sums[j] = tuple(
                (y[2 * i].astype(F32) + swap(y[2 * i + 1], "ctx", 1).astype(F32)).astype(BF16)
                for y in (low, high)
            )
        return [token]

    sums, cots, hiddens = {}, [], []
    token = experts([0], straight, None)
    for j in corners:
        ready = after(corner_half[j], *token)
        other_half = swap(ready, "ep", 1)
        near[j] = (ready, other_half)
        far[j] = (swap(ready, "ctx", 1), swap(other_half, "ctx", 1))
    for j in sides:
        far[j] = (swap(near[j][0], "ctx", 1),) * 2
    own = edge_state(after(seg_col, *token), keys, values, tok - 1, 0, 1)
    fwd = all_states(own, chips)
    for j in corners:
        token = experts([j], turned, token)
    extra = {}
    for j in corners:
        extra[2] = (swap(sums[j][0], "ctx", 2 * 1), None)
        extra[1] = (None, swap(sums[j][1], "ctx", 2 * 2))
        token = [*token, *sums[j]]
    for i in range(0, len(sides), 2):
        token = experts(sides[i : i + 2], straight, token)
    loads = [(near if r % 2 == 0 else far)[r // 2][0] for r in range(shards)]
    weights = state_weights(me, loads, tok)

    part = width // (2 * groups)
    totals, spreads = [], []
    for c in range(2):
        sends = []
        for j in sides:
            send = sums[j][c]
            if j in extra and extra[j][c] is not None:
                send = (send.astype(F32) + extra[j][c].astype(F32)).astype(BF16)
            sends.append(swap(send, "ctx", 2 * j))
        total = sums[0][c].astype(F32)
        sends = lax.optimization_barrier((*sends, *totals))[: len(sides)]
        for x in sends:
            total = total + x.astype(F32)
        total = total.astype(BF16)
        totals.append(total)
        pieces = []
        for j in range(1, groups):
            piece = lax.dynamic_slice_in_dim(total, (place ^ j) * part, part, 1)
            pieces.append(swap(piece, "ep", j))
        spreads.append(pieces)
    down_grad = dot(jnp.concatenate(hiddens), jnp.concatenate(cots), (0, 0))

    dq, dk_dv, before = None, [], [totals[1]]
    for c in range(2):
        pieces = lax.optimization_barrier((*spreads[c], *before))[: groups - 1]
        y_grad = lax.dynamic_slice_in_dim(totals[c], place * part, part, 1).astype(F32)
        for x in pieces:
            y_grad = y_grad + x.astype(F32)
        head_cot = y_grad.astype(BF16)
        own = edge_state(seg_col, queries, head_cot, 0, c, 2)
        back = all_states(own, chips)
        dq, dk, dv = inner_grads(
            weights, seg_col, seg_row, queries, keys, values, head_cot, fwd, c, 2, dq
        )
        before = [own, dk]
        dk_dv = outer_grads(weights, seg_col, keys, values, dk, dv, back, c, 2, dk_dv)
    return (dq, *dk_dv, down_grad[None])


def solution(mesh):
    return jax.shard_map(
        local,
        mesh=mesh,
        in_specs=(
            P("ctx", None),
            P("ctx", None),
            P("ctx", None),
            P("ctx"),
            P(("ctx", "ep"), None, None, None),
            P(("ctx", "ep"), None, None, None),
            P(("ctx", "ep"), None, None),
            P(("ctx", "ep"), None, None),
            P(("ctx", "ep"), None, None),
            P("ctx", "ep"),
            P("ctx", "ep"),
            P("ctx", "ep"),
        ),
        out_specs=(P("ctx", "ep"), P("ctx", "ep"), P("ctx", "ep"), P(("ctx", "ep"), None, None)),
        check_vma=False,
    )
```

time: 393 us -> 195 us (0.50)
  waiting for transfers between devices: 172 us -> 73.6 us
  local copies, waits for them, and re-layouts: 78.5 us -> 5.9 us
  Pallas kernels: 0 us -> 56.1 us
  matrix products: 39.1 us -> 8.23 us
  other arithmetic: 39.4 us -> 13.7 us
  starting transfers between devices: 15.3 us -> 36.1 us
  loops' own time: 18 us -> 0 us
  between operations: 17.3 us -> 1 us
  blocking collectives: 12.7 us -> 0 us
    all_to_all x3 -> x0, waiting for transfers between devices: 142 us -> none  [the longest x1 71.5 us: local(): lax.all_to_all(send_rows, 'ctx', split_axis=0, concat_axis=0, tiled=True)]
    ppermute x0 -> x50, waiting for transfers between devices: none -> 73.6 us  [swap(): lax.ppermute(x, axis, [(i, i ^ offset) for i in range(lax.axis_size(axis))])]
    pallas_call x0 -> x12, Pallas kernels: none -> 56.1 us  [the longest x3 35.4 us: expert_group(): pl.pallas_call(functools.partial(expert_kernel, count=count, groups=group...]
    ppermute x0 -> x50, starting transfers between devices: none -> 36.1 us  [swap(): lax.ppermute(x, axis, [(i, i ^ offset) for i in range(lax.axis_size(axis))])]
    dot_general x14 -> x1, matrix products: 39.1 us -> 8.23 us  [dot(): lax.dot_general(a, b, ((dims[:1], dims[1:]), ((), ())), preferred_element...]
    gather x2 -> x0, local copies, waits for them, and re-layouts: 27.1 us -> none  [the longest x1 20 us: gather_back(): jnp.take(returned.reshape(-1, model_width), row_index, axis=0)]
    scatter x2 -> x0, local copies, waits for them, and re-layouts: 22.6 us -> none  [the longest x1 14.6 us: local(): slot_gate = jnp.zeros((dump_slot,), gate_values.dtype).at[position].set(g...]
    another operation x2 -> x0, loops' own time: 18 us -> none  [prefix(): return lax.fori_loop(0, ahead, one, state)]
  transfers between devices with their start and end apart: 6 -> 50, of which waited for: 4 -> 13; matrix products, arithmetic and copies ran while one was open for 12% -> 12% of each run, Pallas kernels for 0% -> 17%
where the time goes in v1:
time: 195 us
  waiting for transfers between devices  73.6 us (38%)
  Pallas kernels  56.1 us (29%)
  starting transfers between devices  36.1 us (19%)
  other arithmetic  13.7 us (7%)
  matrix products  8.23 us (4%)
  local copies, waits for them, and re-layouts  5.9 us (3%)
    ppermute x50, waiting for transfers between devices, swap(): lax.ppermute(x, axis, [(i, i ^ offset) for i in range(lax.axis_size(axis))])  73.6 us
    ppermute x50, starting transfers between devices, swap(): lax.ppermute(x, axis, [(i, i ^ offset) for i in range(lax.axis_size(axis))])  36.1 us
    pallas_call x3, Pallas kernels, expert_group(): pl.pallas_call(functools.partial(expert_kernel, count=count, groups=group...  35.4 us
    dot_general x1, matrix products, dot(): lax.dot_general(a, b, ((dims[:1], dims[1:]), ((), ())), preferred_element...  8.23 us
    convert_element_type x4, other arithmetic, experts(): (y[2 * i].astype(F32) + swap(y[2 * i + 1], 'ctx', 1).astype(F32)).astype(...  6.63 us
    pallas_call x3, Pallas kernels, edge_state(): pl.pallas_call(functools.partial(state_kernel, edge=edge, heads=heads), g...  6.03 us
    pallas_call x2, Pallas kernels, inner_grads(): pl.pallas_call(functools.partial(inner_kernel, shards=shards, tok=tok, he...  5.75 us
    pallas_call x2, Pallas kernels, outer_grads(): pl.pallas_call(functools.partial(outer_kernel, shards=shards, tok=tok, he...  4.71 us
  transfers between devices with their start and end apart: 50, of which 13 were waited for; matrix products, arithmetic and copies ran while one was open for 12% of the time, Pallas kernels for 17%

profile of v1, /device:TPU:0, one launch (start us, length us, event | category | flops | bytes accessed | tf_op | source)
XLA Modules:
  0.0 194.7 jit_solution(9489221209113413209)
XLA Ops:
  0.6 2.5 %make_load.1 = (bf16[264,2048]{1,0:T(8,128)(2,1)}, bf16[264,1024]{1,0:T(8,128)(2,1)}, f32[256,1]{1,0:T(8,128)}) custom-call(s32[1]{0:T(128)} %bitcast.1.scal, bf16[256,2048]{1,0:T(8,128)(2,1)} %rows.1, bf16[8,256]{1,0:T(8,128)(2,1)} %bitcast.51, s32[8,256]{1,0:T(8,128)} %bitcast.50, s32[1,256]{1,0:T(1,128)} %bitcast.22), custom_call_target="tpu_custom_call" | custom-call | flops 1400000000 | bytes 65536 | tf_op jit(solution)/shard_map/make_load/pallas_call | solution.py:323
  3.7 2.5 %collective-permute-start.1 = (bf16[264,2048]{1,0:T(8,128)(2,1)}, bf16[264,2048]{1,0:T(8,128)(2,1)S(1)}, u32[]{:S(2)}, u32[]{:S(2)}) collective-permute-start(bf16[264,2048]{1,0:T(8,128)(2,1)} %get-tuple-element.54.refs_0_.refs_2_.refs_4_), channel_id=1, source_target_pairs={{0,8},{4,12},{8,0},{12,4},{16,24},{20,28},{24,16},{28,20},{1,9},{5... | collective-permute-start | bytes 3244040 | tf_op jit(solution)/shard_map/ppermute | solution.py:21
  6.1 1.5 collective-permute-start.3
  9.3 9.9 %expert_group.3 = (bf16[256,1024]{1,0:T(8,128)(2,1)}, bf16[256,1024]{1,0:T(8,128)(2,1)}, bf16[256,1024]{1,0:T(8,128)(2,1)}, bf16[256,1024]{1,0:T(8,128)(2,1)}, b...) custom-call(s32[5]{0:T(128)} %stack.42.scal, ...), custom_call_target="tpu_custom_call" | custom-call | flops 6442450944 | bytes 3145728 | tf_op jit(solution)/shard_map/expert_group/pallas_call | solution.py:121
  19.2 24.7 %collective-permute-done.5.refs_6_.refs_0_.refs_2_ = bf16[264,1024]{1,0:T(8,128)(2,1)} collective-permute-done((bf16[264,1024]{1,0:T(8,128)(2,1)}, bf16[264,1024]{1,0:T(8,128)(2,1)}, u32[]{:S(2)}, u32[]{:S(2)}) %collective-permute-start.5) | collective-permute-done | bytes 540704 | tf_op jit(solution)/shard_map/ppermute | solution.py:21
  43.9 1.6 collective-permute-start.8
  45.5 12.5 %collective-permute-done.8.refs_4_ = bf16[264,1024]{1,0:T(8,128)(2,1)} collective-permute-done((bf16[264,1024]{1,0:T(8,128)(2,1)}, bf16[264,1024]{1,0:T(8,128)(2,1)}, u32[]{:S(2)}, u32[]{:S(2)}) %collective-permute-start.8) | collective-permute-done | bytes 540704 | tf_op jit(solution)/shard_map/ppermute | solution.py:21
  60.2 10.0 %expert_group.4 = (bf16[256,1024]{1,0:T(8,128)(2,1)}, bf16[256,1024]{1,0:T(8,128)(2,1)}, bf16[256,1024]{1,0:T(8,128)(2,1)}, bf16[256,1024]{1,0:T(8,128)(2,1)}, b...) custom-call(s32[5]{0:T(128)} %stack.51.scal, ...), custom_call_target="tpu_custom_call" | custom-call | flops 6442450944 | bytes 3145728 | tf_op jit(solution)/shard_map/expert_group/pallas_call | solution.py:121
  72.6 2.2 %add_convert_fusion.9 = bf16[256,1024]{1,0:T(8,128)(2,1)} fusion(bf16[256,1024]{1,0:T(8,128)(2,1)} %collective-permute-done.11, bf16[256,1024]{1,0:T(8,128)(2,1)} %get-tuple-element.64), kind=kLoop, calls=%fused_computation.21 | loop fusion | flops 1048576 | bytes 1572864 | tf_op jit(solution)/shard_map/convert_element_type | solution.py:421
  74.7 2.2 %add_convert_fusion.10 = bf16[256,1024]{1,0:T(8,128)(2,1)} fusion(bf16[256,1024]{1,0:T(8,128)(2,1)} %collective-permute-done.10, bf16[256,1024]{1,0:T(8,128)(2,1)} %get-tuple-element.62), kind=kLoop, calls=%fused_computation.22 | loop fusion | flops 1048576 | bytes 1572864 | tf_op jit(solution)/shard_map/convert_element_type | solution.py:421
  78.0 15.5 %expert_group.5 = (bf16[256,1024]{1,0:T(8,128)(2,1)}, bf16[256,1024]{1,0:T(8,128)(2,1)}, bf16[256,1024]{1,0:T(8,128)(2,1)}, bf16[256,1024]{1,0:T(8,128)(2,1)}, b...) custom-call(s32[7]{0:T(128)} %stack.47.scal, ...), custom_call_target="tpu_custom_call" | custom-call | flops 12884901888 | bytes 6291456 | tf_op jit(solution)/shard_map/expert_group/pallas_call | solution.py:121
  97.5 10.4 %collective-permute-done.21 = bf16[256,1024]{1,0:T(8,128)(2,1)S(1)} collective-permute-done((bf16[256,1024]{1,0:T(8,128)(2,1)S(1)}, bf16[256,1024]{1,0:T(8,128)(2,1)S(1)}, u32[]{:S(2)}, u32[]{:S(2)}) %collective-permute-start.21) | collective-permute-done | bytes 524320 | tf_op jit(solution)/shard_map/ppermute | solution.py:21
  109.4 2.2 %add_convert_fusion.2 = bf16[256,1024]{1,0:T(8,128)(2,1)} fusion(bf16[256,1024]{1,0:T(8,128)(2,1)S(1)} %collective-permute-done.21, bf16[256,1024]{1,0:T(8,128)(2,1)S(1)} %collective-permute-done.20, bf16[256,1024]{1,0:T(8,128)(2,1)} %get-tuple-element.75), kind=kLoop, calls=%fused_computation.14 | loop fusion | flops 2097152 | bytes 2097152 | tf_op jit(solution)/shard_map/convert_element_type | solution.py:456
  116.8 5.9 %collective-permute-done.19 = bf16[256,1024]{1,0:T(8,128)(2,1)S(1)} collective-permute-done((bf16[256,1024]{1,0:T(8,128)(2,1)S(1)}, bf16[256,1024]{1,0:T(8,128)(2,1)S(1)}, u32[]{:S(2)}, u32[]{:S(2)}) %collective-permute-start.19) | collective-permute-done | bytes 524320 | tf_op jit(solution)/shard_map/ppermute | solution.py:21
  122.7 2.1 %edge_state.4 = bf16[4,128,128]{2,1,0:T(8,128)(2,1)} custom-call(f32[256,1]{1,0:T(8,128)} %get-tuple-element.84.seg.seg_col, bf16[256,512]{1,0:T(8,128)(2,1)} %k.7, bf16[256,512]{1,0:T(8,128)(2,1)} %v.7), custom_call_target="tpu_custom_call" | custom-call | flops 700000000 | bytes 65536 | tf_op jit(solution)/shard_map/edge_state/pallas_call | solution.py:189
  124.8 1.7 state_weights.1.weights
  128.9 5.0 %collective-permute-done.14 = bf16[256,1024]{1,0:T(8,128)(2,1)S(1)} collective-permute-done((bf16[256,1024]{1,0:T(8,128)(2,1)}, bf16[256,1024]{1,0:T(8,128)(2,1)S(1)}, u32[]{:S(2)}, u32[]{:S(2)}) %collective-permute-start.14) | collective-permute-done | bytes 524320 | tf_op jit(solution)/shard_map/ppermute | solution.py:21
  135.4 5.2 %collective-permute-done.16 = bf16[256,1024]{1,0:T(8,128)(2,1)S(1)} collective-permute-done((bf16[256,1024]{1,0:T(8,128)(2,1)}, bf16[256,1024]{1,0:T(8,128)(2,1)S(1)}, u32[]{:S(2)}, u32[]{:S(2)}) %collective-permute-start.16) | collective-permute-done | bytes 524320 | tf_op jit(solution)/shard_map/ppermute | solution.py:21
  140.7 1.6 collective-permute-start.26
  142.3 2.6 %collective-permute-start.27 = (bf16[256,256]{1,0:T(8,128)(2,1)S(1)}, bf16[256,256]{1,0:T(8,128)(2,1)S(1)}, u32[]{:S(2)}, u32[]{:S(2)}) collective-permute-start(bf16[256,256]{1,0:T(8,128)(2,1)S(1)} %get-tuple-element.105), channel_id=1, source_target_pairs={{0,2},{1,3},{2,0},{3,1},{4,6},{5,7},{6,4},{7,5},{8,10},{9,11},{10,... | collective-permute-start | bytes 393224 | tf_op jit(solution)/shard_map/ppermute | solution.py:21
  148.0 1.8 collective-permute-done.27
  149.8 2.0 %collective-permute-done.28 = bf16[256,256]{1,0:T(8,128)(2,1)S(1)} collective-permute-done((bf16[256,256]{1,0:T(8,128)(2,1)S(1)}, bf16[256,256]{1,0:T(8,128)(2,1)S(1)}, u32[]{:S(2)}, u32[]{:S(2)}) %collective-permute-start.28) | collective-permute-done | bytes 131104 | tf_op jit(solution)/shard_map/ppermute | solution.py:21
  155.0 1.9 collective-permute-start.25
  157.6 2.9 %inner_grads.2 = (bf16[256,512]{1,0:T(8,128)(2,1)}, f32[256,256]{1,0:T(8,128)}, f32[256,256]{1,0:T(8,128)}) custom-call(f32[8,128]{1,0:T(8,128)} %state_weights.1.weights, f32[256,1]{1,0:T(8,128)} %get-tuple-element.84.seg.seg_col, f32[1,256]{1,0:T(1,128)} %bitcast.23, bf16[256,512]{1,0:T(8,128)(2,1)} %left.5, bf16[256,512]{1,0:T(8,128)(2,1)} %k.7, ...), custom_call_target="tpu_custom_call" | custom-call | flops 2100000000 | bytes 65536 | tf_op jit(solution)/shard_map/inner_grads/pallas_call | solution.py:252
  160.4 2.0 %edge_state.3 = bf16[2,128,128]{2,1,0:T(8,128)(2,1)} custom-call(f32[256,1]{1,0:T(8,128)} %get-tuple-element.84.seg.seg_col, bf16[256,512]{1,0:T(8,128)(2,1)} %left.5, bf16[256,256]{1,0:T(8,128)(2,1)} %add_convert_fusion.13.right.g), custom_call_target="tpu_custom_call" | custom-call | flops 700000000 | bytes 65536 | tf_op jit(solution)/shard_map/edge_state/pallas_call | solution.py:189
  162.4 3.0 %collective-permute-done.24 = bf16[256,256]{1,0:T(8,128)(2,1)S(1)} collective-permute-done((bf16[256,256]{1,0:T(8,128)(2,1)S(1)}, bf16[256,256]{1,0:T(8,128)(2,1)S(1)}, u32[]{:S(2)}, u32[]{:S(2)}) %collective-permute-start.24) | collective-permute-done | bytes 131104 | tf_op jit(solution)/shard_map/ppermute | solution.py:21
  166.2 2.0 %edge_state.5 = bf16[2,128,128]{2,1,0:T(8,128)(2,1)} custom-call(f32[256,1]{1,0:T(8,128)} %get-tuple-element.84.seg.seg_col, bf16[256,512]{1,0:T(8,128)(2,1)} %left.5, bf16[256,256]{1,0:T(8,128)(2,1)} %add_convert_fusion.12.g.right), custom_call_target="tpu_custom_call" | custom-call | flops 700000000 | bytes 65536 | tf_op jit(solution)/shard_map/edge_state/pallas_call | solution.py:189
  173.3 8.2 %fusion.6 = f32[1,512,2048]{2,1,0:T(8,128)} fusion(bf16[768,2048]{1,0:T(8,128)(2,1)} %get-tuple-element.103, bf16[384,2048]{1,0:T(8,128)(2,1)} %get-tuple-element.102, bf16[384,2048]{1,0:T(8,128)(2,1)S(1)} %copy-done.34, bf16[768,512]{1,0:T(8,128)(2,1)} %get-tuple-element.100, bf16[384,512]{1,0:T(8,128)(2,1)} %get-tuple-element.99, ...), kind=kOutput, calls=%fused_computation.6 | convolution fusion | flops 3244818432 | bytes 12058624 | tf_op jit(solution)/shard_map/dot_general | solution.py:17
  181.5 1.9 collective-permute-start.41
  184.5 2.9 %inner_grads.3 = (bf16[256,512]{1,0:T(8,128)(2,1)}, f32[256,256]{1,0:T(8,128)}, f32[256,256]{1,0:T(8,128)}) custom-call(f32[8,128]{1,0:T(8,128)} %state_weights.1.weights, f32[256,1]{1,0:T(8,128)} %get-tuple-element.84.seg.seg_col, f32[1,256]{1,0:T(1,128)} %bitcast.24, bf16[256,512]{1,0:T(8,128)(2,1)} %left.5, ...), custom_call_target="tpu_custom_call", output_to_operand_aliasing={{0}: (14, {})} | custom-call | flops 2100000000 | bytes 65536 | tf_op jit(solution)/shard_map/inner_grads/pallas_call | solution.py:252
  189.2 2.4 %outer_grads.2 = (bf16[256,512]{1,0:T(8,128)(2,1)}, bf16[256,512]{1,0:T(8,128)(2,1)}) custom-call(f32[8,128]{1,0:T(8,128)} %state_weights.1.weights, f32[256,1]{1,0:T(8,128)} %get-tuple-element.84.seg.seg_col, bf16[256,512]{1,0:T(8,128)(2,1)} %k.7, bf16[256,512]{1,0:T(8,128)(2,1)} %v.7, f32[256,256]{1,0:T(8,128)} %get-tuple-element.85.dk_in, ...), custom_call_target="tpu_custom_call" | custom-call | flops 1400000000 | bytes 65536 | tf_op jit(solution)/shard_map/outer_grads/pallas_call | solution.py:283
  192.3 2.4 %outer_grads.3 = (bf16[256,512]{1,0:T(8,128)(2,1)}, bf16[256,512]{1,0:T(8,128)(2,1)}) custom-call(f32[8,128]{1,0:T(8,128)} %state_weights.1.weights, f32[256,1]{1,0:T(8,128)} %get-tuple-element.84.seg.seg_col, bf16[256,512]{1,0:T(8,128)(2,1)} %k.7, bf16[256,512]{1,0:T(8,128)(2,1)} %v.7, ...), custom_call_target="tpu_custom_call", output_to_operand_aliasing={{0}: (13, {}), {1}: (14, {})} | custom-call | flops 1400000000 | bytes 65536 | tf_op jit(solution)/shard_map/outer_grads/pallas_call | solution.py:283
  (169 shorter events, 38.7 us)
Async XLA Ops:
  3.7 54.9 %collective-permute-start.1 = (bf16[264,2048]{1,0:T(8,128)(2,1)}, bf16[264,2048]{1,0:T(8,128)(2,1)S(1)}, u32[]{:S(2)}, u32[]{:S(2)}) collective-permute-start(bf16[264,2048]{1,0:T(8,128)(2,1)} %get-tuple-element.54.refs_0_.refs_2_.refs_4_), channel_id=1, source_target_pairs={{0,8},{4,12},{8,0},{12,4},{16,24},{20,28},{24,16},{28,20},{1,9},{5... | collective-permute-start | bytes 3244040 | tf_op jit(solution)/shard_map/ppermute | solution.py:21
  6.1 53.0 %collective-permute-start.3 = (bf16[264,2048]{1,0:T(8,128)(2,1)}, bf16[264,2048]{1,0:T(8,128)(2,1)S(1)}, u32[]{:S(2)}, u32[]{:S(2)}) collective-permute-start(bf16[264,2048]{1,0:T(8,128)(2,1)} %get-tuple-element.54.refs_0_.refs_2_.refs_4_), channel_id=1, source_target_pairs={{0,16},{4,20},{8,24},{12,28},{16,0},{20,4},{24,8},{28,12},{1,17},{... | collective-permute-start | bytes 3244040 | tf_op jit(solution)/shard_map/ppermute | solution.py:21
  7.6 36.2 %collective-permute-start.5 = (bf16[264,1024]{1,0:T(8,128)(2,1)}, bf16[264,1024]{1,0:T(8,128)(2,1)}, u32[]{:S(2)}, u32[]{:S(2)}) collective-permute-start(bf16[264,1024]{1,0:T(8,128)(2,1)} %get-tuple-element.55), channel_id=1, source_target_pairs={{0,24},{4,28},{8,16},{12,20},{16,8},{20,12},{24,0},{28,4},{1,25},{... | collective-permute-start | bytes 1622024 | tf_op jit(solution)/shard_map/ppermute | solution.py:21
  43.9 14.1 %collective-permute-start.8 = (bf16[264,1024]{1,0:T(8,128)(2,1)}, bf16[264,1024]{1,0:T(8,128)(2,1)}, u32[]{:S(2)}, u32[]{:S(2)}) collective-permute-start(bf16[264,1024]{1,0:T(8,128)(2,1)} %collective-permute-done.5.refs_6_.refs_0_.refs_2_), channel_id=1, source_target_pairs={{0,1},{1,0},{2,3},{3,2},{4,5},{5,4},{6,7},{7,6},{8,9},{9,8},{10,11... | collective-permute-start | bytes 1622024 | tf_op jit(solution)/shard_map/ppermute | solution.py:21
  45.4 13.7 %collective-permute-start.6 = (bf16[264,1024]{1,0:T(8,128)(2,1)}, bf16[264,1024]{1,0:T(8,128)(2,1)}, u32[]{:S(2)}, u32[]{:S(2)}) collective-permute-start(bf16[264,1024]{1,0:T(8,128)(2,1)} %collective-permute-done.5.refs_6_.refs_0_.refs_2_), channel_id=1, source_target_pairs={{0,4},{4,0},{8,12},{12,8},{16,20},{20,16},{24,28},{28,24},{1,5},{5... | collective-permute-start | bytes 1622024 | tf_op jit(solution)/shard_map/ppermute | solution.py:21
  58.6 18.4 %collective-permute-start.2 = (bf16[264,2048]{1,0:T(8,128)(2,1)S(1)}, bf16[264,2048]{1,0:T(8,128)(2,1)S(1)}, u32[]{:S(2)}, u32[]{:S(2)}) collective-permute-start(bf16[264,2048]{1,0:T(8,128)(2,1)S(1)} %collective-permute-done.1.refs_2_.refs_0_.refs_4_.refs_8_), channel_id=1, source_target_pairs={{0,4},{4,0},{8,12},{12,8},{16,20},{20,16},{24,28},{28,24},{1,5},{5... | collective-permute-start | bytes 3244040 | tf_op jit(solution)/shard_map/ppermute | solution.py:21
  59.1 17.9 %collective-permute-start.4 = (bf16[264,2048]{1,0:T(8,128)(2,1)S(1)}, bf16[264,2048]{1,0:T(8,128)(2,1)}, u32[]{:S(2)}, u32[]{:S(2)}) collective-permute-start(bf16[264,2048]{1,0:T(8,128)(2,1)S(1)} %collective-permute-done.3.refs_4_.refs_2_.refs_6_.refs_10_), channel_id=1, source_target_pairs={{0,4},{4,0},{8,12},{12,8},{16,20},{20,16},{24,28},{28,24},{1,5},{5... | collective-permute-start | bytes 3244040 | tf_op jit(solution)/shard_map/ppermute | solution.py:21
  93.7 14.2 %collective-permute-start.21 = (bf16[256,1024]{1,0:T(8,128)(2,1)S(1)}, bf16[256,1024]{1,0:T(8,128)(2,1)S(1)}, u32[]{:S(2)}, u32[]{:S(2)}) collective-permute-start(bf16[256,1024]{1,0:T(8,128)(2,1)S(1)} %copy-done.7), channel_id=1, source_target_pairs={{0,8},{4,12},{8,0},{12,4},{16,24},{20,28},{24,16},{28,20},{1,9},{5... | collective-permute-start | bytes 1572872 | tf_op jit(solution)/shard_map/ppermute | solution.py:21
  95.2 12.7 %collective-permute-start.20 = (bf16[256,1024]{1,0:T(8,128)(2,1)}, bf16[256,1024]{1,0:T(8,128)(2,1)S(1)}, u32[]{:S(2)}, u32[]{:S(2)}) collective-permute-start(bf16[256,1024]{1,0:T(8,128)(2,1)} %get-tuple-element.76), channel_id=1, source_target_pairs={{0,4},{4,0},{8,12},{12,8},{16,20},{20,16},{24,28},{28,24},{1,5},{5... | collective-permute-start | bytes 1572872 | tf_op jit(solution)/shard_map/ppermute | solution.py:21
  95.2 32.8 %collective-permute-start.17 = (bf16[256,1024]{1,0:T(8,128)(2,1)}, bf16[256,1024]{1,0:T(8,128)(2,1)S(1)}, u32[]{:S(2)}, u32[]{:S(2)}) collective-permute-start(bf16[256,1024]{1,0:T(8,128)(2,1)} %get-tuple-element.72), channel_id=1, source_target_pairs={{0,4},{4,0},{8,12},{12,8},{16,20},{20,16},{24,28},{28,24},{1,5},{5... | collective-permute-start | bytes 1572872 | tf_op jit(solution)/shard_map/ppermute | solution.py:21
  95.7 15.9 %collective-permute-start.13 = (bf16[256,1024]{1,0:T(8,128)(2,1)}, bf16[256,1024]{1,0:T(8,128)(2,1)S(1)}, u32[]{:S(2)}, u32[]{:S(2)}) collective-permute-start(bf16[256,1024]{1,0:T(8,128)(2,1)} %add_convert_fusion.9), channel_id=1, source_target_pairs={{0,16},{4,20},{8,24},{12,28},{16,0},{20,4},{24,8},{28,12},{1,17},{... | collective-permute-start | bytes 1572872 | tf_op jit(solution)/shard_map/ppermute | solution.py:21
  96.2 15.9 %collective-permute-start.12 = (bf16[256,1024]{1,0:T(8,128)(2,1)}, bf16[256,1024]{1,0:T(8,128)(2,1)S(1)}, u32[]{:S(2)}, u32[]{:S(2)}) collective-permute-start(bf16[256,1024]{1,0:T(8,128)(2,1)} %get-tuple-element.68), channel_id=1, source_target_pairs={{0,4},{4,0},{8,12},{12,8},{16,20},{20,16},{24,28},{28,24},{1,5},{5... | collective-permute-start | bytes 1572872 | tf_op jit(solution)/shard_map/ppermute | solution.py:21
  107.9 14.8 %collective-permute-start.19 = (bf16[256,1024]{1,0:T(8,128)(2,1)S(1)}, bf16[256,1024]{1,0:T(8,128)(2,1)S(1)}, u32[]{:S(2)}, u32[]{:S(2)}) collective-permute-start(bf16[256,1024]{1,0:T(8,128)(2,1)S(1)} %add_convert_fusion.4), channel_id=1, source_target_pairs={{0,8},{4,12},{8,0},{12,4},{16,24},{20,28},{24,16},{28,20},{1,9},{5... | collective-permute-start | bytes 1572872 | tf_op jit(solution)/shard_map/ppermute | solution.py:21
  111.5 15.0 %collective-permute-start.22 = (bf16[256,1024]{1,0:T(8,128)(2,1)}, bf16[256,1024]{1,0:T(8,128)(2,1)S(1)}, u32[]{:S(2)}, u32[]{:S(2)}) collective-permute-start(bf16[256,1024]{1,0:T(8,128)(2,1)} %add_convert_fusion.2), channel_id=1, source_target_pairs={{0,16},{4,20},{8,24},{12,28},{16,0},{20,4},{24,8},{28,12},{1,17},{... | collective-permute-start | bytes 1572872 | tf_op jit(solution)/shard_map/ppermute | solution.py:21
  113.2 20.8 %collective-permute-start.14 = (bf16[256,1024]{1,0:T(8,128)(2,1)}, bf16[256,1024]{1,0:T(8,128)(2,1)S(1)}, u32[]{:S(2)}, u32[]{:S(2)}) collective-permute-start(bf16[256,1024]{1,0:T(8,128)(2,1)} %add_convert_fusion.7), channel_id=1, source_target_pairs={{0,8},{4,12},{8,0},{12,4},{16,24},{20,28},{24,16},{28,20},{1,9},{5... | collective-permute-start | bytes 1572872 | tf_op jit(solution)/shard_map/ppermute | solution.py:21
  114.7 25.9 %collective-permute-start.16 = (bf16[256,1024]{1,0:T(8,128)(2,1)}, bf16[256,1024]{1,0:T(8,128)(2,1)S(1)}, u32[]{:S(2)}, u32[]{:S(2)}) collective-permute-start(bf16[256,1024]{1,0:T(8,128)(2,1)} %add_convert_fusion.6), channel_id=1, source_target_pairs={{0,16},{4,20},{8,24},{12,28},{16,0},{20,4},{24,8},{28,12},{1,17},{... | collective-permute-start | bytes 1572872 | tf_op jit(solution)/shard_map/ppermute | solution.py:21
  122.7 22.2 %collective-permute-start.7 = (bf16[256,1024]{1,0:T(8,128)(2,1)}, bf16[256,1024]{1,0:T(8,128)(2,1)}, u32[]{:S(2)}, u32[]{:S(2)}) collective-permute-start(bf16[256,1024]{1,0:T(8,128)(2,1)} %get-tuple-element.60), channel_id=1, source_target_pairs={{0,4},{4,0},{8,12},{12,8},{16,20},{20,16},{24,28},{28,24},{1,5},{5... | collective-permute-start | bytes 1572872 | tf_op jit(solution)/shard_map/ppermute | solution.py:21
  126.6 15.7 %collective-permute-start.30 = (bf16[4,128,128]{2,1,0:T(8,128)(2,1)S(1)}, bf16[4,128,128]{2,1,0:T(8,128)(2,1)S(1)}, u32[]{:S(2)}, u32[]{:S(2)}) collective-permute-start(bf16[4,128,128]{2,1,0:T(8,128)(2,1)S(1)} %copy-done.17), channel_id=1, source_target_pairs={{0,8},{4,12},{8,0},{12,4},{16,24},{20,28},{24,16},{28,20},{1,9},{5... | collective-permute-start | bytes 393224 | tf_op jit(solution)/shard_map/ppermute | solution.py:21
  128.0 18.6 %collective-permute-start.32 = (bf16[4,128,128]{2,1,0:T(8,128)(2,1)S(1)}, bf16[4,128,128]{2,1,0:T(8,128)(2,1)S(1)}, u32[]{:S(2)}, u32[]{:S(2)}) collective-permute-start(bf16[4,128,128]{2,1,0:T(8,128)(2,1)S(1)} %copy-done.17), channel_id=1, source_target_pairs={{0,16},{4,20},{8,24},{12,28},{16,0},{20,4},{24,8},{28,12},{1,17},{... | collective-permute-start | bytes 393224 | tf_op jit(solution)/shard_map/ppermute | solution.py:21
  133.9 12.8 %collective-permute-start.34 = (bf16[4,128,128]{2,1,0:T(8,128)(2,1)S(1)}, bf16[4,128,128]{2,1,0:T(8,128)(2,1)S(1)}, u32[]{:S(2)}, u32[]{:S(2)}) collective-permute-start(bf16[4,128,128]{2,1,0:T(8,128)(2,1)S(1)} %copy-done.17), channel_id=1, source_target_pairs={{0,24},{4,28},{8,16},{12,20},{16,8},{20,12},{24,0},{28,4},{1,25},{... | collective-permute-start | bytes 393224 | tf_op jit(solution)/shard_map/ppermute | solution.py:21
  140.7 7.3 %collective-permute-start.26 = (bf16[256,256]{1,0:T(8,128)(2,1)S(1)}, bf16[256,256]{1,0:T(8,128)(2,1)S(1)}, u32[]{:S(2)}, u32[]{:S(2)}) collective-permute-start(bf16[256,256]{1,0:T(8,128)(2,1)S(1)} %get-tuple-element.106), channel_id=1, source_target_pairs={{0,1},{1,0},{2,3},{3,2},{4,5},{5,4},{6,7},{7,6},{8,9},{9,8},{10,11... | collective-permute-start | bytes 393224 | tf_op jit(solution)/shard_map/ppermute | solution.py:21
  142.3 7.5 %collective-permute-start.27 = (bf16[256,256]{1,0:T(8,128)(2,1)S(1)}, bf16[256,256]{1,0:T(8,128)(2,1)S(1)}, u32[]{:S(2)}, u32[]{:S(2)}) collective-permute-start(bf16[256,256]{1,0:T(8,128)(2,1)S(1)} %get-tuple-element.105), channel_id=1, source_target_pairs={{0,2},{1,3},{2,0},{3,1},{4,6},{5,7},{6,4},{7,5},{8,10},{9,11},{10,... | collective-permute-start | bytes 393224 | tf_op jit(solution)/shard_map/ppermute | solution.py:21
  146.7 8.3 %collective-permute-start.31 = (bf16[4,128,128]{2,1,0:T(8,128)(2,1)S(1)}, bf16[4,128,128]{2,1,0:T(8,128)(2,1)S(1)}, u32[]{:S(2)}, u32[]{:S(2)}) collective-permute-start(bf16[4,128,128]{2,1,0:T(8,128)(2,1)S(1)} %collective-permute-done.30.refs_1_), channel_id=1, source_target_pairs={{0,4},{4,0},{8,12},{12,8},{16,20},{20,16},{24,28},{28,24},{1,5},{5... | collective-permute-start | bytes 393224 | tf_op jit(solution)/shard_map/ppermute | solution.py:21
  148.0 8.9 %collective-permute-start.33 = (bf16[4,128,128]{2,1,0:T(8,128)(2,1)S(1)}, bf16[4,128,128]{2,1,0:T(8,128)(2,1)S(1)}, u32[]{:S(2)}, u32[]{:S(2)}) collective-permute-start(bf16[4,128,128]{2,1,0:T(8,128)(2,1)S(1)} %collective-permute-done.32.refs_3_), channel_id=1, source_target_pairs={{0,4},{4,0},{8,12},{12,8},{16,20},{20,16},{24,28},{28,24},{1,5},{5... | collective-permute-start | bytes 393224 | tf_op jit(solution)/shard_map/ppermute | solution.py:21
  151.7 10.7 %collective-permute-start.23 = (bf16[256,256]{1,0:T(8,128)(2,1)S(1)}, bf16[256,256]{1,0:T(8,128)(2,1)S(1)}, u32[]{:S(2)}, u32[]{:S(2)}) collective-permute-start(bf16[256,256]{1,0:T(8,128)(2,1)S(1)} %get-tuple-element.109), channel_id=1, source_target_pairs={{0,1},{1,0},{2,3},{3,2},{4,5},{5,4},{6,7},{7,6},{8,9},{9,8},{10,11... | collective-permute-start | bytes 393224 | tf_op jit(solution)/shard_map/ppermute | solution.py:21
  153.8 11.6 %collective-permute-start.24 = (bf16[256,256]{1,0:T(8,128)(2,1)S(1)}, bf16[256,256]{1,0:T(8,128)(2,1)S(1)}, u32[]{:S(2)}, u32[]{:S(2)}) collective-permute-start(bf16[256,256]{1,0:T(8,128)(2,1)S(1)} %get-tuple-element.108), channel_id=1, source_target_pairs={{0,2},{1,3},{2,0},{3,1},{4,6},{5,7},{6,4},{7,5},{8,10},{9,11},{10,... | collective-permute-start | bytes 393224 | tf_op jit(solution)/shard_map/ppermute | solution.py:21
  155.0 10.4 %collective-permute-start.25 = (bf16[256,256]{1,0:T(8,128)(2,1)S(1)}, bf16[256,256]{1,0:T(8,128)(2,1)S(1)}, u32[]{:S(2)}, u32[]{:S(2)}) collective-permute-start(bf16[256,256]{1,0:T(8,128)(2,1)S(1)} %get-tuple-element.107), channel_id=1, source_target_pairs={{0,3},{1,2},{2,1},{3,0},{4,7},{5,6},{6,5},{7,4},{8,11},{9,10},{10,... | collective-permute-start | bytes 393224 | tf_op jit(solution)/shard_map/ppermute | solution.py:21
  168.1 13.4 %collective-permute-start.37 = (bf16[2,128,128]{2,1,0:T(8,128)(2,1)}, bf16[2,128,128]{2,1,0:T(8,128)(2,1)S(1)}, u32[]{:S(2)}, u32[]{:S(2)}) collective-permute-start(bf16[2,128,128]{2,1,0:T(8,128)(2,1)} %edge_state.5), channel_id=1, source_target_pairs={{0,8},{4,12},{8,0},{12,4},{16,24},{20,28},{24,16},{28,20},{1,9},{5... | collective-permute-start | bytes 196616 | tf_op jit(solution)/shard_map/ppermute | solution.py:21
  169.2 14.2 %collective-permute-start.39 = (bf16[2,128,128]{2,1,0:T(8,128)(2,1)}, bf16[2,128,128]{2,1,0:T(8,128)(2,1)S(1)}, u32[]{:S(2)}, u32[]{:S(2)}) collective-permute-start(bf16[2,128,128]{2,1,0:T(8,128)(2,1)} %edge_state.5), channel_id=1, source_target_pairs={{0,16},{4,20},{8,24},{12,28},{16,0},{20,4},{24,8},{28,12},{1,17},{... | collective-permute-start | bytes 196616 | tf_op jit(solution)/shard_map/ppermute | solution.py:21
  169.8 13.7 %collective-permute-start.44 = (bf16[2,128,128]{2,1,0:T(8,128)(2,1)S(1)}, bf16[2,128,128]{2,1,0:T(8,128)(2,1)S(1)}, u32[]{:S(2)}, u32[]{:S(2)}) collective-permute-start(bf16[2,128,128]{2,1,0:T(8,128)(2,1)S(1)} %copy-done.22), channel_id=1, source_target_pairs={{0,8},{4,12},{8,0},{12,4},{16,24},{20,28},{24,16},{28,20},{1,9},{5... | collective-permute-start | bytes 196616 | tf_op jit(solution)/shard_map/ppermute | solution.py:21
  170.7 13.2 %collective-permute-start.46 = (bf16[2,128,128]{2,1,0:T(8,128)(2,1)S(1)}, bf16[2,128,128]{2,1,0:T(8,128)(2,1)S(1)}, u32[]{:S(2)}, u32[]{:S(2)}) collective-permute-start(bf16[2,128,128]{2,1,0:T(8,128)(2,1)S(1)} %copy-done.22), channel_id=1, source_target_pairs={{0,16},{4,20},{8,24},{12,28},{16,0},{20,4},{24,8},{28,12},{1,17},{... | collective-permute-start | bytes 196616 | tf_op jit(solution)/shard_map/ppermute | solution.py:21
  172.2 11.9 %collective-permute-start.48 = (bf16[2,128,128]{2,1,0:T(8,128)(2,1)S(1)}, bf16[2,128,128]{2,1,0:T(8,128)(2,1)S(1)}, u32[]{:S(2)}, u32[]{:S(2)}) collective-permute-start(bf16[2,128,128]{2,1,0:T(8,128)(2,1)S(1)} %copy-done.22), channel_id=1, source_target_pairs={{0,24},{4,28},{8,16},{12,20},{16,8},{20,12},{24,0},{28,4},{1,25},{... | collective-permute-start | bytes 196616 | tf_op jit(solution)/shard_map/ppermute | solution.py:21
  (54 other events, 285.5 us)

commit v2 on v1

--- a/solution.py
+++ b/solution.py
@@ -21,17 +21,13 @@
     return lax.ppermute(x, axis, [(i, i ^ offset) for i in range(lax.axis_size(axis))])
 
 
-def after(x, *others):
-    return lax.optimization_barrier((x, *others))[0]
-
-
-def expert_kernel(scal, *refs, count, groups, tok, slots):
+def expert_kernel(scal, *refs, count, skip, groups, tok, slots):
     routes, refs = refs[:count], refs[count:]
-    early, refs = refs[:count], refs[count:]
-    late, refs = refs[:count], refs[count:]
+    quarters, refs = [refs[q * count : (q + 1) * count] for q in range(4)], refs[4 * count :]
     pres, refs = refs[:count], refs[count:]
     ups, refs = refs[:count], refs[count:]
     w_down, w_gate, w_up = refs[:3]
+    refs = refs[skip:]
     lows, highs = refs[3 : 3 + count], refs[3 + count : 3 + 2 * count]
     cot, hidden, token, pick, back, part, gate_delta, up_delta = refs[3 + 2 * count :]
     step = pl.program_id(0)
@@ -55,18 +51,21 @@
             pick[i] = (chosen * gate).astype(BF16)
             back[i] = chosen.T.astype(BF16)
 
-    def gather(rows):
-        for i in range(count):
-            cot[i * slots : (i + 1) * slots, :] = dot(pick[i], rows[i][...], (1, 0)).astype(BF16)
+    def gather(*rows):
+        quarter = cot.shape[1] // 2
+        for q in range(2):
+            for i in range(count):
+                here = (slice(i * slots, (i + 1) * slots), slice(q * quarter, (q + 1) * quarter))
+                cot[here] = dot(pick[i], rows[q][i][...], (1, 0)).astype(BF16)
         return dot(cot[...], w_down[...], (1, 1))
 
     @pl.when(step == 0)
     def _():
-        part[...] = gather(early)
+        part[...] = gather(*quarters[:2])
 
     @pl.when(step == 1)
     def _():
-        part[...] += gather(late)
+        part[...] += gather(*quarters[2:])
         for i in range(count):
             here = pl.ds(i * slots, slots)
             a = pres[i][0].astype(F32)
@@ -90,11 +89,11 @@
                 highs[i][:, there] = y[:, (2 * g + 1) * half : (2 * g + 2) * half]
 
 
-def expert_group(scal, loads, gate_pre, up_pre, w_gate, w_up, w_down, groups):
+def expert_group(scal, sources, order, tokens, loads, gate_pre, up_pre, weights, groups):
     _, slots, ffp = gate_pre.shape
     count = len(loads)
-    tok = loads[0][0].shape[0] - 8
-    width = w_gate.shape[0]
+    tok = loads[0][0][0].shape[0] - 8
+    width = weights[0].shape[1]
     chunk = width // 2
 
     def early(i):
@@ -103,30 +102,30 @@
     def late(i):
         return jnp.maximum(i - 2, 0)
 
-    route = pl.BlockSpec((8, 4 * tok), lambda i, s: (tok // 8, 0))
-    first = pl.BlockSpec((tok, chunk), lambda i, s: (0, 0))
-    seconds = [
-        pl.BlockSpec((tok, chunk), functools.partial(lambda i, s, skip: (0, skip), skip=b.shape[1] // chunk - 1))
-        for a, b in loads
+    route = pl.BlockSpec((8, 2 * tok), lambda i, s: (tok // 8, 0))
+    rows = [
+        pl.BlockSpec((tok, chunk // 2), functools.partial(lambda i, s, block: (0, block), block=load[q][1]))
+        for q in range(4)
+        for load in loads
     ]
     pres = [
-        pl.BlockSpec((1, slots, ffp), functools.partial(lambda i, s, n: (s[1 + n], 0, 0), n=n))
-        for n in range(count)
+        pl.BlockSpec((1, slots, ffp), functools.partial(lambda i, s, n: (s[n], 0, 0), n=n))
+        for n in sources
     ]
-    down = pl.BlockSpec((ffp, chunk), lambda i, s: (0, s[1 + count + early(i)]))
+    down = pl.BlockSpec((ffp, chunk), lambda i, s: (0, s[order + early(i)]))
     up = pl.BlockSpec((chunk, ffp), lambda i, s: (late(i), 0))
     y = pl.BlockSpec((tok, chunk // 2), lambda i, s: (0, late(i)))
-    half_rows = jax.ShapeDtypeStruct((tok, width // 2), BF16)
+    half_rows = pltpu.HBM((tok, width // 2), BF16)
     m = count * slots
     outs = pl.pallas_call(
-        functools.partial(expert_kernel, count=count, groups=groups, tok=tok, slots=slots),
+        functools.partial(expert_kernel, count=count, skip=len(tokens), groups=groups, tok=tok, slots=slots),
         grid_spec=pltpu.PrefetchScalarGridSpec(
             num_scalar_prefetch=1,
             grid=(4,),
-            in_specs=[route] * count + [first] * count + seconds + pres * 2 + [down, up, up],
+            in_specs=[route] * count + rows + pres * 2 + [down, up, up] + [pl.BlockSpec(memory_space=pl.ANY)] * len(tokens),
             out_specs=[y] * (2 * count)
             + [
-                pl.BlockSpec((m, chunk), lambda i, s: (0, s[1 + count + early(i)])),
+                pl.BlockSpec((m, chunk), lambda i, s: (0, s[order + early(i)])),
                 pl.BlockSpec((m, ffp), lambda i, s: (0, 0)),
                 pl.BlockSpec((8, 128), lambda i, s: (0, 0)),
             ],
@@ -140,24 +139,23 @@
         ),
         out_shape=[half_rows] * (2 * count)
         + [
-            jax.ShapeDtypeStruct((m, width), BF16),
-            jax.ShapeDtypeStruct((m, ffp), BF16),
+            pltpu.HBM((m, width), BF16),
+            pltpu.HBM((m, ffp), BF16),
             jax.ShapeDtypeStruct((8, 128), F32),
         ],
         cost_estimate=pl.CostEstimate(
             flops=4 * m * width * (3 * ffp + 2 * tok), transcendentals=m * ffp, bytes_accessed=4 * m * width
         ),
+        compiler_params=pltpu.CompilerParams(vmem_limit_bytes=(4 + 13 * count) << 20),
         name="expert_group",
     )(
         scal,
-        *[a for a, b in loads],
-        *[a for a, b in loads],
-        *[b for a, b in loads],
-        *[gate_pre] * count,
-        *[up_pre] * count,
-        w_down,
-        w_gate,
-        w_up,
+        *[load[0][0] for load in loads],
+        *[load[q][0] for q in range(4) for load in loads],
+        *[pltpu.with_memory_space_constraint(gate_pre, pltpu.HBM)] * count,
+        *[pltpu.with_memory_space_constraint(up_pre, pltpu.HBM)] * count,
+        *weights,
+        *tokens,
     )
     return outs[:count], outs[count : 2 * count], *outs[-3:]
 
@@ -170,31 +168,68 @@
     return ref[:, h * HEAD_DIM : (h + 1) * HEAD_DIM]
 
 
-def state_kernel(seg, left, right, out, *, edge, heads):
+def put_states(seg, left, right, out, edge, heads):
     keep = seg[...] == seg[edge : edge + 1, :]
     rows = jnp.where(keep, left[...].astype(F32), 0.0).astype(BF16)
     for h in range(heads):
-        out[h] = dot(head_of(rows, h), head_of(right, h), (0, 0)).astype(BF16)
+        out[h] = dot(head_of(rows, h), right[:, h * HEAD_DIM : (h + 1) * HEAD_DIM], (0, 0)).astype(BF16)
+
+
+def forward_kernel(seg, left, right, out, *, edge, heads):
+    put_states(seg, left, right, out, edge, heads)
+
+
+def backward_kernel(scal, seg, left, *refs, heads):
+    right, out = refs[-2:]
+    right[...] = sum(x[...].astype(F32) for x in refs[:-2]).astype(BF16)
+    put_states(seg, left, right, out, 0, heads)
 
 
 def columns(x, part, parts):
     return pl.BlockSpec((x.shape[0], x.shape[1] // parts), lambda i: (0, part))
 
 
-def edge_state(seg_col, left, right, edge, part, parts):
-    wide = left.shape[1] // parts
-    heads = wide // HEAD_DIM
-    whole = pl.BlockSpec((heads, HEAD_DIM, HEAD_DIM), lambda i: (0, 0, 0))
-    right_parts = right.shape[1] // wide
+def forward_states(seg_col, left, right):
+    tok, width = left.shape
+    heads = width // HEAD_DIM
     return pl.pallas_call(
-        functools.partial(state_kernel, edge=edge, heads=heads),
+        functools.partial(forward_kernel, edge=tok - 1, heads=heads),
         grid=(1,),
-        in_specs=[columns(seg_col, 0, 1), columns(left, part, parts), columns(right, part % right_parts, right_parts)],
-        out_specs=whole,
+        in_specs=[columns(x, 0, 1) for x in (seg_col, left, right)],
+        out_specs=pl.BlockSpec((heads, HEAD_DIM, HEAD_DIM), lambda i: (0, 0, 0)),
         out_shape=jax.ShapeDtypeStruct((heads, HEAD_DIM, HEAD_DIM), BF16),
         cost_estimate=small_cost(1),
-        name="edge_state",
+        compiler_params=pltpu.CompilerParams(vmem_limit_bytes=8 << 20),
+        name="forward_states",
     )(seg_col, left, right)
+
+
+def backward_states(place, seg_col, left, total, pieces, part, parts):
+    tok, width = left.shape
+    wide = width // parts
+    heads = wide // HEAD_DIM
+    own = pl.BlockSpec((tok, wide), lambda i, s: (0, 0))
+    return pl.pallas_call(
+        functools.partial(backward_kernel, heads=heads),
+        grid_spec=pltpu.PrefetchScalarGridSpec(
+            num_scalar_prefetch=1,
+            grid=(1,),
+            in_specs=[
+                pl.BlockSpec((tok, 1), lambda i, s: (0, 0)),
+                pl.BlockSpec((tok, wide), lambda i, s: (0, part)),
+                pl.BlockSpec((tok, wide), lambda i, s: (0, s[0])),
+                *[own] * len(pieces),
+            ],
+            out_specs=[own, pl.BlockSpec((heads, HEAD_DIM, HEAD_DIM), lambda i, s: (0, 0, 0))],
+        ),
+        out_shape=[
+            jax.ShapeDtypeStruct((tok, wide), BF16),
+            jax.ShapeDtypeStruct((heads, HEAD_DIM, HEAD_DIM), BF16),
+        ],
+        cost_estimate=small_cost(1),
+        compiler_params=pltpu.CompilerParams(vmem_limit_bytes=8 << 20),
+        name="backward_states",
+    )(place[None], seg_col, left, total, *pieces)
 
 
 def weighted(weights, side, states, shards):
@@ -268,6 +303,7 @@
         ],
         input_output_aliases={6 + shards: 0} if filled else {},
         cost_estimate=small_cost(3),
+        compiler_params=pltpu.CompilerParams(vmem_limit_bytes=8 << 20),
         name="inner_grads",
     )(weights, seg_col, seg_row, q, k, v, g, *states, *filled)
 
@@ -294,23 +330,33 @@
         out_shape=[jax.ShapeDtypeStruct((tok, width), BF16)] * 2,
         input_output_aliases={5 + shards: 0, 6 + shards: 1} if filled else {},
         cost_estimate=small_cost(2),
+        compiler_params=pltpu.CompilerParams(vmem_limit_bytes=8 << 20),
         name="outer_grads",
     )(weights, seg_col, k, v, dk, dv, *states, *filled)
 
 
-def load_kernel(scal, rows, gates, ids, seg, load, half, seg_col, *, tok, width):
-    start = pl.multiple_of(scal[0] * (width // 2), width // 2)
+def load_kernel(scal, rows, gates, ids, seg, load, low, high, seg_col, seg_row, *, tok, width):
+    quarter = width // 4
+    start = pl.multiple_of(scal[0] * 2 * quarter, 2 * quarter)
     load[:tok, :] = rows[...]
-    half[:tok, :] = rows[:, pl.ds(start, width // 2)]
-    gate_rows = gates[...].astype(F32)
-    id_rows = ids[...].astype(F32)
-    seg_rows = jnp.broadcast_to(seg[...].astype(F32), (128, tok))
+    low[:tok, :] = rows[:, pl.ds(start, quarter)]
+    high[:tok, :] = rows[:, pl.ds(start + quarter, quarter)]
+    segment = seg[...].astype(F32)
+    seg_rows = jnp.broadcast_to(segment, (128, tok))
     seg_col[...] = seg_rows.T[:, :1]
-    rest = jnp.zeros((8, width // 2 - 3 * tok), F32)
-    route = jnp.concatenate([gate_rows, id_rows, seg_rows[:8], rest], axis=1).astype(BF16)
-    load[tok:, : width // 2] = route
-    load[tok:, width // 2 :] = route
-    half[tok:, :] = route
+    seg_row[...] = segment
+
+    def padded(*parts):
+        spare = quarter - sum(x.shape[1] for x in parts)
+        parts += (jnp.zeros((8, spare), F32),) if spare else ()
+        return jnp.concatenate(parts, axis=1).astype(BF16)
+
+    route = padded(gates[...].astype(F32), ids[...].astype(F32))
+    seg_part = padded(seg_rows[:8])
+    for q in range(4):
+        load[tok:, q * quarter : (q + 1) * quarter] = seg_part if q % 2 else route
+    low[tok:, :] = route
+    high[tok:, :] = seg_part
 
 
 def make_load(parity, rows, gates, ids, seg):
@@ -319,7 +365,7 @@
     def whole(shape):
         return pl.BlockSpec(shape, lambda i, s: (0, 0))
 
-    shapes = [(tok + 8, width), (tok + 8, width // 2), (tok, 1)]
+    shapes = [(tok + 8, width), (tok + 8, width // 4), (tok + 8, width // 4), (tok, 1), (1, tok)]
     return pl.pallas_call(
         functools.partial(load_kernel, tok=tok, width=width),
         grid_spec=pltpu.PrefetchScalarGridSpec(
@@ -328,7 +374,7 @@
             in_specs=[whole(x.shape) for x in (rows, gates, ids, seg)],
             out_specs=[whole(x) for x in shapes],
         ),
-        out_shape=[jax.ShapeDtypeStruct(x, t) for x, t in zip(shapes, (BF16, BF16, F32))],
+        out_shape=[jax.ShapeDtypeStruct(x, t) for x, t in zip(shapes, (BF16, BF16, BF16, F32, F32))],
         cost_estimate=small_cost(2),
         name="make_load",
     )(parity[None], rows, gates, ids, seg)
@@ -337,15 +383,15 @@
 def weight_kernel(scal, *refs, shards, tok):
     routes, out = refs[:shards], refs[shards]
     me = scal[0]
-    first = routes[0][:1, 2 * tok : 2 * tok + 1].astype(F32)
-    last = routes[0][:1, 3 * tok - 1 : 3 * tok].astype(F32)
+    first = routes[0][:1, :1].astype(F32)
+    last = routes[0][:1, tok - 1 : tok].astype(F32)
     side = lax.broadcasted_iota(jnp.int32, (8, 128), 0)
     lane = lax.broadcasted_iota(jnp.int32, (8, 128), 1)
     total = jnp.zeros((8, 128), F32)
     for r in range(1, shards):
         other = me ^ r
-        first_r = routes[r][:1, 2 * tok : 2 * tok + 1].astype(F32)
-        last_r = routes[r][:1, 3 * tok - 1 : 3 * tok].astype(F32)
+        first_r = routes[r][:1, :1].astype(F32)
+        last_r = routes[r][:1, tok - 1 : tok].astype(F32)
         earlier = (last_r == first) & (other < me) & (side == 0)
         later = (first_r == last) & (other > me) & (side == 1)
         total = jnp.where((lane == r) & (earlier | later), 1.0, total)
@@ -359,19 +405,28 @@
         grid_spec=pltpu.PrefetchScalarGridSpec(
             num_scalar_prefetch=1,
             grid=(1,),
-            in_specs=[pl.BlockSpec((8, 4 * tok), lambda i, s: (tok // 8, 0))] * shards,
+            in_specs=[
+                pl.BlockSpec(
+                    (8, tok), functools.partial(lambda i, s, block: (tok // 8, block), block=b // tok)
+                )
+                for x, b in loads
+            ],
             out_specs=pl.BlockSpec((8, 128), lambda i, s: (0, 0)),
         ),
         out_shape=jax.ShapeDtypeStruct((8, 128), F32),
         cost_estimate=small_cost(1),
+        compiler_params=pltpu.CompilerParams(vmem_limit_bytes=8 << 20),
         name="state_weights",
-    )(me[None], *loads)
-
-
-def all_states(own, chips):
-    near = [own] + [swap(own, "ctx", 2 * j) for j in range(1, chips)]
+    )(me[None], *[x for x, b in loads])
+
+
+def near_states(own, chips):
+    return [own] + [swap(own, "ctx", 2 * j) for j in range(1, chips)]
+
+
+def all_states(near):
     far = [swap(x, "ctx", 1) for x in near]
-    return [(near if r % 2 == 0 else far)[r // 2] for r in range(1, 2 * chips)]
+    return [(near if r % 2 == 0 else far)[r // 2] for r in range(1, 2 * len(near))]
 
 
 def local(
@@ -388,74 +443,73 @@
     expert = 2 * me + place // (groups // 2)
     corners = [3] if chips == 4 else []
     sides = [j for j in range(1, chips) if j not in corners]
-    weights3 = (w_gate[0], w_up[0], w_down[0])
-
-    seg_row = segment_ids[None, :]
-    load, mine, seg_col = make_load(parity, out_grad, gate_values.T, expert_ids.T, seg_row)
-    seg_row = seg_row.astype(F32)
-    near = {0: (load, load)}
-    far = {}
-    corner_half = {j: swap(mine, "ctx", 2 * j) for j in corners}
-    far[0] = (swap(load, "ctx", 1),) * 2
+    weights3 = [pltpu.with_memory_space_constraint(x[0], pltpu.VMEM) for x in (w_down, w_gate, w_up)]
+
+    load, low, high, seg_col, seg_row = make_load(
+        parity, out_grad, gate_values.T, expert_ids.T, segment_ids[None, :]
+    )
+
+    def whole(x):
+        return [(x, q) for q in range(4)]
+
+    near, far = {0: whole(load)}, {}
+    corner_half = {j: [swap(x, "ctx", 2 * j) for x in (low, high)] for j in corners}
+    far[0] = whole(swap(load, "ctx", 1))
     for j in sides:
-        near[j] = (swap(load, "ctx", 2 * j),) * 2
-
-    straight = [jnp.int32(0), jnp.int32(1)]
-    turned = [parity, 1 - parity]
-
-    def experts(js, order, token):
+        near[j] = whole(swap(load, "ctx", 2 * j))
+
+    scal = jnp.stack([expert] + [me ^ r for r in range(shards)] + [me * 0, me * 0 + 1, parity, 1 - parity])
+    straight, turned = shards + 1, shards + 3
+
+    def experts(js, order, tokens):
         loads, sources = [], []
         for j in js:
             loads += [near[j], far[j]]
-            sources += [me ^ (2 * j), me ^ (2 * j + 1)]
-        scal = jnp.stack([expert, *sources, *order])
-        if token is not None:
-            scal = after(scal, *token)
+            sources += [1 + 2 * j, 2 + 2 * j]
         low, high, cot, hidden, token = expert_group(
-            scal, loads, gate_pre[0], up_pre[0], *weights3, groups
+            scal, sources, order, tokens, loads, gate_pre[0], up_pre[0], weights3, groups
         )
         cots.append(cot)
         hiddens.append(hidden)
         for i, j in enumerate(js):
-            sums[j] = tuple(
-                (y[2 * i].astype(F32) + swap(y[2 * i + 1], "ctx", 1).astype(F32)).astype(BF16)
-                for y in (low, high)
-            )
+            sums[j] = [[y[2 * i], swap(y[2 * i + 1], "ctx", 1)] for y in (low, high)]
         return [token]
 
+    def added(xs):
+        return sum(x.astype(F32) for x in xs).astype(BF16)
+
     sums, cots, hiddens = {}, [], []
-    token = experts([0], straight, None)
     for j in corners:
-        ready = after(corner_half[j], *token)
-        other_half = swap(ready, "ep", 1)
-        near[j] = (ready, other_half)
-        far[j] = (swap(ready, "ctx", 1), swap(other_half, "ctx", 1))
+        first, second = corner_half[j]
+        third = swap(first, "ep", 1)
+        fourth = swap(second, "ep", 1)
+        near[j] = [(x, 0) for x in (first, second, third, fourth)]
+        far[j] = [(swap(x, "ctx", 1), 0) for x, _ in near[j]]
     for j in sides:
-        far[j] = (swap(near[j][0], "ctx", 1),) * 2
-    own = edge_state(after(seg_col, *token), keys, values, tok - 1, 0, 1)
-    fwd = all_states(own, chips)
+        far[j] = whole(swap(near[j][0][0], "ctx", 1))
+    own = forward_states(seg_col, keys, values)
+    fwd_near = near_states(own, chips)
+    token = experts([0], straight, [])
     for j in corners:
         token = experts([j], turned, token)
     extra = {}
-    for j in corners:
-        extra[2] = (swap(sums[j][0], "ctx", 2 * 1), None)
-        extra[1] = (None, swap(sums[j][1], "ctx", 2 * 2))
-        token = [*token, *sums[j]]
-    for i in range(0, len(sides), 2):
-        token = experts(sides[i : i + 2], straight, token)
-    loads = [(near if r % 2 == 0 else far)[r // 2][0] for r in range(shards)]
-    weights = state_weights(me, loads, tok)
+    for i, j in enumerate(sides):
+        token = experts([j], straight, token)
+        if i == 0:
+            for k in corners:
+                rows = [added(lax.optimization_barrier((*x, *token))[:2]) for x in sums[k]]
+                extra[2] = ([swap(rows[0], "ctx", 2 * 1)], [])
+                extra[1] = ([], [swap(rows[1], "ctx", 2 * 2)])
+                token = [*token, *rows]
+    loads = [(near if r % 2 == 0 else far)[r // 2][1] for r in range(shards)]
+    weights = state_weights(me, [(x, b * (width // 4)) for x, b in loads], tok)
 
     part = width // (2 * groups)
     totals, spreads = [], []
     for c in range(2):
-        sends = []
-        for j in sides:
-            send = sums[j][c]
-            if j in extra and extra[j][c] is not None:
-                send = (send.astype(F32) + extra[j][c].astype(F32)).astype(BF16)
-            sends.append(swap(send, "ctx", 2 * j))
-        total = sums[0][c].astype(F32)
+        rows = [added(sums[j][c] + extra.get(j, ([], []))[c]) for j in sides]
+        sends = [swap(x, "ctx", 2 * j) for j, x in zip(sides, rows)]
+        total = sums[0][c][0].astype(F32) + sums[0][c][1].astype(F32)
         sends = lax.optimization_barrier((*sends, *totals))[: len(sides)]
         for x in sends:
             total = total + x.astype(F32)
@@ -468,15 +522,12 @@
         spreads.append(pieces)
     down_grad = dot(jnp.concatenate(hiddens), jnp.concatenate(cots), (0, 0))
 
+    fwd = all_states(lax.optimization_barrier((*fwd_near, totals[1]))[:chips])
     dq, dk_dv, before = None, [], [totals[1]]
     for c in range(2):
         pieces = lax.optimization_barrier((*spreads[c], *before))[: groups - 1]
-        y_grad = lax.dynamic_slice_in_dim(totals[c], place * part, part, 1).astype(F32)
-        for x in pieces:
-            y_grad = y_grad + x.astype(F32)
-        head_cot = y_grad.astype(BF16)
-        own = edge_state(seg_col, queries, head_cot, 0, c, 2)
-        back = all_states(own, chips)
+        head_cot, own = backward_states(place, seg_col, queries, totals[c], pieces, c, 2)
+        back = all_states(near_states(own, chips))
         dq, dk, dv = inner_grads(
             weights, seg_col, seg_row, queries, keys, values, head_cot, fwd, c, 2, dq
         )

time: 195 us -> 190 us (0.974)
  Pallas kernels: 56.1 us -> 44.2 us
  waiting for transfers between devices: 73.6 us -> 83.3 us
  other arithmetic: 13.7 us -> 7.95 us
  starting transfers between devices: 36.1 us -> 39 us
  matrix products: 8.23 us -> 5.62 us
  local copies, waits for them, and re-layouts: 5.9 us -> 8.35 us
    ppermute x50 -> x54, waiting for transfers between devices: 73.6 us -> 83.3 us  [swap(): lax.ppermute(x, axis, [(i, i ^ offset) for i in range(lax.axis_size(axis))])]
    convert_element_type x9 -> x6, other arithmetic: 11.9 us -> 4.57 us  [added(): return sum((x.astype(F32) for x in xs)).astype(BF16)]
    pallas_call x6 -> x7, Pallas kernels: 41.4 us -> 35.6 us  [the longest x4 34.6 us: expert_group(): pl.pallas_call(functools.partial(expert_kernel, count=count, skip=len(tok...]
    unnamed x72 -> x74, local copies, waits for them, and re-layouts: 3.98 us -> 8.16 us
    pallas_call x2, Pallas kernels: 5.75 us -> 2.87 us  [inner_grads(): pl.pallas_call(functools.partial(inner_kernel, shards=shards, tok=tok, he...]
    ppermute x50 -> x54, starting transfers between devices: 36.1 us -> 39 us  [swap(): lax.ppermute(x, axis, [(i, i ^ offset) for i in range(lax.axis_size(axis))])]
    dot_general x1, matrix products: 8.23 us -> 5.62 us  [dot(): lax.dot_general(a, b, ((dims[:1], dims[1:]), ((), ())), preferred_element...]
    pallas_call x2, Pallas kernels: 4.71 us -> 2.15 us  [outer_grads(): pl.pallas_call(functools.partial(outer_kernel, shards=shards, tok=tok, he...]
  transfers between devices with their start and end apart: 50 -> 54, of which waited for: 13 -> 11; matrix products, arithmetic and copies ran while one was open for 12% -> 7% of each run, Pallas kernels for 17% -> 21%
where the time goes in v2:
time: 190 us
  waiting for transfers between devices  83.3 us (44%)
  Pallas kernels  44.2 us (23%)
  starting transfers between devices  39 us (21%)
  local copies, waits for them, and re-layouts  8.35 us (4%)
  other arithmetic  7.95 us (4%)
  matrix products  5.62 us (3%)
    ppermute x54, waiting for transfers between devices, swap(): lax.ppermute(x, axis, [(i, i ^ offset) for i in range(lax.axis_size(axis))])  83.3 us
    ppermute x54, starting transfers between devices, swap(): lax.ppermute(x, axis, [(i, i ^ offset) for i in range(lax.axis_size(axis))])  39 us
    pallas_call x4, Pallas kernels, expert_group(): pl.pallas_call(functools.partial(expert_kernel, count=count, skip=len(tok...  34.6 us
    unnamed x74, local copies, waits for them, and re-layouts  8.16 us
    dot_general x1, matrix products, dot(): lax.dot_general(a, b, ((dims[:1], dims[1:]), ((), ())), preferred_element...  5.62 us
    convert_element_type x6, other arithmetic, added(): return sum((x.astype(F32) for x in xs)).astype(BF16)  4.57 us
  transfers between devices with their start and end apart: 54, of which 11 were waited for; matrix products, arithmetic and copies ran while one was open for 7% of the time, Pallas kernels for 21%

profile of v2, /device:TPU:0, one launch (start us, length us, event | category | flops | bytes accessed | tf_op | source)
XLA Modules:
  0.0 189.5 jit_solution(7615146777793922017)
XLA Ops:
  0.7 2.6 %make_load.1 = (bf16[264,2048]{1,0:T(8,128)(2,1)}, bf16[264,512]{1,0:T(8,128)(2,1)}, bf16[264,512]{1,0:T(8,128)(2,1)}, f32[256,1]{1,0:T(8,128)}, f32[1,256]{1,0:T(1,128)}) custom-call(s32[1]{0:T(128)} %bitcast.1.scal, bf16[256,2048]{1,0:T(8,128)(2,1)} %rows.1, bf16[8,256]{1,0:T(8,128)(2,1)} %bitcast.51, s32[8,256]{1,0:T(8,128)} %bitcast.50, s32[1,256]{1,0:T(1,128)} %bitcast.52), custom_call_target="tpu_custom_call" | custom-call | flops 1400000000 | bytes 65536 | tf_op jit(solution)/shard_map/make_load/pallas_call | solution.py:369
  3.8 2.5 %collective-permute-start.1 = (bf16[264,2048]{1,0:T(8,128)(2,1)}, bf16[264,2048]{1,0:T(8,128)(2,1)}, u32[]{:S(2)}, u32[]{:S(2)}) collective-permute-start(bf16[264,2048]{1,0:T(8,128)(2,1)} %get-tuple-element.68.refs_0_.refs_2_.refs_4_.refs_6_.refs_8_), channel_id=1, source_target_pairs={{0,8},{4,12},{8,0},{12,4},{16,24},{20,28},{24,16},{28,20},{1,9},{5... | collective-permute-start | bytes 3244040 | tf_op jit(solution)/shard_map/ppermute | solution.py:21
  9.2 29.3 %collective-permute-done.5.refs_6_.refs_4_ = bf16[264,512]{1,0:T(8,128)(2,1)S(1)} collective-permute-done((bf16[264,512]{1,0:T(8,128)(2,1)}, bf16[264,512]{1,0:T(8,128)(2,1)S(1)}, u32[]{:S(2)}, u32[]{:S(2)}) %collective-permute-start.5) | collective-permute-done | bytes 270368 | tf_op jit(solution)/shard_map/ppermute | solution.py:21
  38.5 5.4 %collective-permute-done.8.refs_0_.refs_2_ = bf16[264,512]{1,0:T(8,128)(2,1)} collective-permute-done((bf16[264,512]{1,0:T(8,128)(2,1)}, bf16[264,512]{1,0:T(8,128)(2,1)}, u32[]{:S(2)}, u32[]{:S(2)}) %collective-permute-start.8) | collective-permute-done | bytes 270368 | tf_op jit(solution)/shard_map/ppermute | solution.py:21
  43.9 1.6 collective-permute-start.10
  47.0 6.6 %collective-permute-done.10.refs_6_ = bf16[264,512]{1,0:T(8,128)(2,1)} collective-permute-done((bf16[264,512]{1,0:T(8,128)(2,1)}, bf16[264,512]{1,0:T(8,128)(2,1)}, u32[]{:S(2)}, u32[]{:S(2)}) %collective-permute-start.10) | collective-permute-done | bytes 270368 | tf_op jit(solution)/shard_map/ppermute | solution.py:21
  53.6 4.4 %collective-permute-done.12.refs_8_ = bf16[264,512]{1,0:T(8,128)(2,1)} collective-permute-done((bf16[264,512]{1,0:T(8,128)(2,1)S(1)}, bf16[264,512]{1,0:T(8,128)(2,1)}, u32[]{:S(2)}, u32[]{:S(2)}) %collective-permute-start.12) | collective-permute-done | bytes 270368 | tf_op jit(solution)/shard_map/ppermute | solution.py:21
  58.6 1.6 copy-done.2
  60.2 1.6 copy-done.3
  63.0 8.6 %expert_group.4 = (bf16[256,1024]{1,0:T(8,128)(2,1)}, bf16[256,1024]{1,0:T(8,128)(2,1)}, bf16[256,1024]{1,0:T(8,128)(2,1)}, bf16[256,1024]{1,0:T(8,128)(2,1)}, b...) custom-call(s32[13]{0:T(128)S(1)} %stack.41.scal, bf16[264,2048]{1,0:T(8,128)(2,1)S(1)} %copy-done.4, ...), custom_call_target="tpu_custom_call" | custom-call | flops 6442450944 | bytes 3145728 | tf_op jit(solution)/shard_map/expert_group/pallas_call | solution.py:120
  71.6 8.6 %expert_group.5 = (bf16[256,1024]{1,0:T(8,128)(2,1)}, bf16[256,1024]{1,0:T(8,128)(2,1)}, bf16[256,1024]{1,0:T(8,128)(2,1)}, bf16[256,1024]{1,0:T(8,128)(2,1)}, b...) custom-call(s32[13]{0:T(128)S(1)} %stack.41.scal, ...), custom_call_target="tpu_custom_call" | custom-call | flops 6442450944 | bytes 3145728 | tf_op jit(solution)/shard_map/expert_group/pallas_call | solution.py:120
  81.2 8.7 %expert_group.6 = (bf16[256,1024]{1,0:T(8,128)(2,1)}, bf16[256,1024]{1,0:T(8,128)(2,1)}, bf16[256,1024]{1,0:T(8,128)(2,1)}, bf16[256,1024]{1,0:T(8,128)(2,1)}, b...) custom-call(s32[13]{0:T(128)S(1)} %stack.41.scal, ...), custom_call_target="tpu_custom_call" | custom-call | flops 6442450944 | bytes 3145728 | tf_op jit(solution)/shard_map/expert_group/pallas_call | solution.py:120
  90.2 1.6 collective-permute-start.25
  92.0 8.8 %expert_group.7 = (bf16[256,1024]{1,0:T(8,128)(2,1)}, bf16[256,1024]{1,0:T(8,128)(2,1)}, bf16[256,1024]{1,0:T(8,128)(2,1)}, bf16[256,1024]{1,0:T(8,128)(2,1)}, b...) custom-call(s32[13]{0:T(128)S(1)} %stack.41.scal, ...), custom_call_target="tpu_custom_call" | custom-call | flops 6442450944 | bytes 3145728 | tf_op jit(solution)/shard_map/expert_group/pallas_call | solution.py:120
  102.9 1.6 collective-permute-done.25
  104.5 1.6 collective-permute-start.23
  107.2 8.1 %collective-permute-done.16 = bf16[256,1024]{1,0:T(8,128)(2,1)S(1)} collective-permute-done((bf16[256,1024]{1,0:T(8,128)(2,1)S(1)}, bf16[256,1024]{1,0:T(8,128)(2,1)S(1)}, u32[]{:S(2)}, u32[]{:S(2)}) %collective-permute-start.16) | collective-permute-done | bytes 524320 | tf_op jit(solution)/shard_map/ppermute | solution.py:21
  118.5 1.5 collective-permute-start.20
  124.3 6.2 %collective-permute-done.26 = bf16[256,1024]{1,0:T(8,128)(2,1)} collective-permute-done((bf16[256,1024]{1,0:T(8,128)(2,1)}, bf16[256,1024]{1,0:T(8,128)(2,1)}, u32[]{:S(2)}, u32[]{:S(2)}) %collective-permute-start.26) | collective-permute-done | bytes 524320 | tf_op jit(solution)/shard_map/ppermute | solution.py:21
  131.5 1.8 add_convert_fusion.1.refs_0_
  133.3 2.5 %collective-permute-start.35 = (bf16[4,128,128]{2,1,0:T(8,128)(2,1)S(1)}, bf16[4,128,128]{2,1,0:T(8,128)(2,1)S(1)}, u32[]{:S(2)}, u32[]{:S(2)}) collective-permute-start(bf16[4,128,128]{2,1,0:T(8,128)(2,1)S(1)} %forward_states.1), channel_id=1, source_target_pairs={{0,24},{4,28},{8,16},{12,20},{16,8},{20,12},{24,0},{28,4},{1,25},{... | collective-permute-start | bytes 393224 | tf_op jit(solution)/shard_map/ppermute | solution.py:21
  135.8 8.5 %collective-permute-done.20 = bf16[256,1024]{1,0:T(8,128)(2,1)} collective-permute-done((bf16[256,1024]{1,0:T(8,128)(2,1)}, bf16[256,1024]{1,0:T(8,128)(2,1)}, u32[]{:S(2)}, u32[]{:S(2)}) %collective-permute-start.20) | collective-permute-done | bytes 524320 | tf_op jit(solution)/shard_map/ppermute | solution.py:21
  144.4 1.6 collective-permute-start.30
  146.0 2.6 %collective-permute-start.31 = (bf16[256,256]{1,0:T(8,128)(2,1)S(1)}, bf16[256,256]{1,0:T(8,128)(2,1)S(1)}, u32[]{:S(2)}, u32[]{:S(2)}) collective-permute-start(bf16[256,256]{1,0:T(8,128)(2,1)S(1)} %get-tuple-element.133), channel_id=1, source_target_pairs={{0,2},{1,3},{2,0},{3,1},{4,6},{5,7},{6,4},{7,5},{8,10},{9,11},{10,... | collective-permute-start | bytes 393224 | tf_op jit(solution)/shard_map/ppermute | solution.py:21
  148.8 1.6 add_convert_fusion.refs_0_
  151.2 5.0 %collective-permute-done.31.refs_2_ = bf16[256,256]{1,0:T(8,128)(2,1)S(1)} collective-permute-done((bf16[256,256]{1,0:T(8,128)(2,1)S(1)}, bf16[256,256]{1,0:T(8,128)(2,1)S(1)}, u32[]{:S(2)}, u32[]{:S(2)}) %collective-permute-start.31) | collective-permute-done | bytes 131104 | tf_op jit(solution)/shard_map/ppermute | solution.py:21
  156.2 1.9 %collective-permute-start.27 = (bf16[256,256]{1,0:T(8,128)(2,1)S(1)}, bf16[256,256]{1,0:T(8,128)(2,1)S(1)}, u32[]{:S(2)}, u32[]{:S(2)}) collective-permute-start(bf16[256,256]{1,0:T(8,128)(2,1)S(1)} %get-tuple-element.137), channel_id=1, source_target_pairs={{0,1},{1,0},{2,3},{3,2},{4,5},{5,4},{6,7},{7,6},{8,9},{9,8},{10,11... | collective-permute-start | bytes 393224 | tf_op jit(solution)/shard_map/ppermute | solution.py:21
  163.8 7.0 %collective-permute-done.28.refs_2_ = bf16[256,256]{1,0:T(8,128)(2,1)S(1)} collective-permute-done((bf16[256,256]{1,0:T(8,128)(2,1)S(1)}, bf16[256,256]{1,0:T(8,128)(2,1)S(1)}, u32[]{:S(2)}, u32[]{:S(2)}) %collective-permute-start.28) | collective-permute-done | bytes 131104 | tf_op jit(solution)/shard_map/ppermute | solution.py:21
  171.7 1.9 %collective-permute-start.48 = (bf16[2,128,128]{2,1,0:T(8,128)(2,1)S(1)}, bf16[2,128,128]{2,1,0:T(8,128)(2,1)S(1)}, u32[]{:S(2)}, u32[]{:S(2)}) collective-permute-start(bf16[2,128,128]{2,1,0:T(8,128)(2,1)S(1)} %get-tuple-element.103), channel_id=1, source_target_pairs={{0,8},{4,12},{8,0},{12,4},{16,24},{20,28},{24,16},{28,20},{1,9},{5... | collective-permute-start | bytes 196616 | tf_op jit(solution)/shard_map/ppermute | solution.py:21
  173.7 1.6 collective-permute-start.50
  175.3 5.6 %fusion.8 = f32[1,512,2048]{2,1,0:T(8,128)} fusion(bf16[384,2048]{1,0:T(8,128)(2,1)S(1)} %copy-done.27, bf16[384,2048]{1,0:T(8,128)(2,1)S(1)} %copy-done.31, bf16[384,2048]{1,0:T(8,128)(2,1)S(1)} %copy-done.35, bf16[384,2048]{1,0:T(8,128)(2,1)S(1)} %copy-done.32, bf16[384,512]{1,0:T(8,128)(2,1)S(1)} %copy-done.30, bf16[384,512]{1,0:T(8,128)(2,1)S(1)} %copy-done.33, ...), kind=kOutput, calls=%fused_computation.8 | convolution fusion | flops 3252682752 | bytes 12058624 | tf_op jit(solution)/shard_map/dot_general | solution.py:17
  180.9 2.9 %collective-permute-start.45 = (bf16[2,128,128]{2,1,0:T(8,128)(2,1)S(1)}, bf16[2,128,128]{2,1,0:T(8,128)(2,1)S(1)}, u32[]{:S(2)}, u32[]{:S(2)}) collective-permute-start(bf16[2,128,128]{2,1,0:T(8,128)(2,1)S(1)} %get-tuple-element.118), channel_id=1, source_target_pairs={{0,24},{4,28},{8,16},{12,20},{16,8},{20,12},{24,0},{28,4},{1,25},{... | collective-permute-start | bytes 196616 | tf_op jit(solution)/shard_map/ppermute | solution.py:21
  (175 shorter events, 33.2 us)
Async XLA Ops:
  3.3 54.7 %collective-permute-start = (bf16[264,2048]{1,0:T(8,128)(2,1)}, bf16[264,2048]{1,0:T(8,128)(2,1)}, u32[]{:S(2)}, u32[]{:S(2)}) collective-permute-start(bf16[264,2048]{1,0:T(8,128)(2,1)} %get-tuple-element.68.refs_0_.refs_2_.refs_4_.refs_6_.refs_8_), channel_id=1, source_target_pairs={{0,4},{4,0},{8,12},{12,8},{16,20},{20,16},{24,28},{28,24},{1,5},{5... | collective-permute-start | bytes 3244040 | tf_op jit(solution)/shard_map/ppermute | solution.py:21
  3.8 54.7 %collective-permute-start.1 = (bf16[264,2048]{1,0:T(8,128)(2,1)}, bf16[264,2048]{1,0:T(8,128)(2,1)}, u32[]{:S(2)}, u32[]{:S(2)}) collective-permute-start(bf16[264,2048]{1,0:T(8,128)(2,1)} %get-tuple-element.68.refs_0_.refs_2_.refs_4_.refs_6_.refs_8_), channel_id=1, source_target_pairs={{0,8},{4,12},{8,0},{12,4},{16,24},{20,28},{24,16},{28,20},{1,9},{5... | collective-permute-start | bytes 3244040 | tf_op jit(solution)/shard_map/ppermute | solution.py:21
  6.3 32.2 %collective-permute-start.5 = (bf16[264,512]{1,0:T(8,128)(2,1)}, bf16[264,512]{1,0:T(8,128)(2,1)S(1)}, u32[]{:S(2)}, u32[]{:S(2)}) collective-permute-start(bf16[264,512]{1,0:T(8,128)(2,1)} %get-tuple-element.69), channel_id=1, source_target_pairs={{0,24},{4,28},{8,16},{12,20},{16,8},{20,12},{24,0},{28,4},{1,25},{... | collective-permute-start | bytes 811016 | tf_op jit(solution)/shard_map/ppermute | solution.py:21
  7.8 36.1 %collective-permute-start.8 = (bf16[264,512]{1,0:T(8,128)(2,1)}, bf16[264,512]{1,0:T(8,128)(2,1)}, u32[]{:S(2)}, u32[]{:S(2)}) collective-permute-start(bf16[264,512]{1,0:T(8,128)(2,1)} %get-tuple-element.74), channel_id=1, source_target_pairs={{0,24},{4,28},{8,16},{12,20},{16,8},{20,12},{24,0},{28,4},{1,25},{... | collective-permute-start | bytes 811016 | tf_op jit(solution)/shard_map/ppermute | solution.py:21
  45.5 12.5 %collective-permute-start.12 = (bf16[264,512]{1,0:T(8,128)(2,1)S(1)}, bf16[264,512]{1,0:T(8,128)(2,1)}, u32[]{:S(2)}, u32[]{:S(2)}) collective-permute-start(bf16[264,512]{1,0:T(8,128)(2,1)S(1)} %collective-permute-done.5.refs_6_.refs_4_), channel_id=1, source_target_pairs={{0,1},{1,0},{2,3},{3,2},{4,5},{5,4},{6,7},{7,6},{8,9},{9,8},{10,11... | collective-permute-start | bytes 811016 | tf_op jit(solution)/shard_map/ppermute | solution.py:21
  46.7 34.0 %collective-permute-start.3 = (bf16[264,2048]{1,0:T(8,128)(2,1)}, bf16[264,2048]{1,0:T(8,128)(2,1)S(1)}, u32[]{:S(2)}, u32[]{:S(2)}) collective-permute-start(bf16[264,2048]{1,0:T(8,128)(2,1)} %get-tuple-element.68.refs_0_.refs_2_.refs_4_.refs_6_.refs_8_), channel_id=1, source_target_pairs={{0,16},{4,20},{8,24},{12,28},{16,0},{20,4},{24,8},{28,12},{1,17},{... | collective-permute-start | bytes 3244040 | tf_op jit(solution)/shard_map/ppermute | solution.py:21
  53.6 18.0 %collective-permute-start.9 = (bf16[264,512]{1,0:T(8,128)(2,1)}, bf16[264,512]{1,0:T(8,128)(2,1)S(1)}, u32[]{:S(2)}, u32[]{:S(2)}) collective-permute-start(bf16[264,512]{1,0:T(8,128)(2,1)} %collective-permute-done.8.refs_0_.refs_2_), channel_id=1, source_target_pairs={{0,4},{4,0},{8,12},{12,8},{16,20},{20,16},{24,28},{28,24},{1,5},{5... | collective-permute-start | bytes 811016 | tf_op jit(solution)/shard_map/ppermute | solution.py:21
  58.0 13.6 %collective-permute-start.11 = (bf16[264,512]{1,0:T(8,128)(2,1)}, bf16[264,512]{1,0:T(8,128)(2,1)S(1)}, u32[]{:S(2)}, u32[]{:S(2)}) collective-permute-start(bf16[264,512]{1,0:T(8,128)(2,1)} %collective-permute-done.10.refs_6_), channel_id=1, source_target_pairs={{0,4},{4,0},{8,12},{12,8},{16,20},{20,16},{24,28},{28,24},{1,5},{5... | collective-permute-start | bytes 811016 | tf_op jit(solution)/shard_map/ppermute | solution.py:21
  58.0 13.6 %collective-permute-start.13 = (bf16[264,512]{1,0:T(8,128)(2,1)}, bf16[264,512]{1,0:T(8,128)(2,1)S(1)}, u32[]{:S(2)}, u32[]{:S(2)}) collective-permute-start(bf16[264,512]{1,0:T(8,128)(2,1)} %collective-permute-done.12.refs_8_), channel_id=1, source_target_pairs={{0,4},{4,0},{8,12},{12,8},{16,20},{20,16},{24,28},{28,24},{1,5},{5... | collective-permute-start | bytes 811016 | tf_op jit(solution)/shard_map/ppermute | solution.py:21
  58.5 22.7 %collective-permute-start.2 = (bf16[264,2048]{1,0:T(8,128)(2,1)}, bf16[264,2048]{1,0:T(8,128)(2,1)S(1)}, u32[]{:S(2)}, u32[]{:S(2)}) collective-permute-start(bf16[264,2048]{1,0:T(8,128)(2,1)} %collective-permute-done.1.refs_2_.refs_0_.refs_4_.refs_6_.refs_8_), channel_id=1, source_target_pairs={{0,4},{4,0},{8,12},{12,8},{16,20},{20,16},{24,28},{28,24},{1,5},{5... | collective-permute-start | bytes 3244040 | tf_op jit(solution)/shard_map/ppermute | solution.py:21
  80.7 11.3 %collective-permute-start.4 = (bf16[264,2048]{1,0:T(8,128)(2,1)S(1)}, bf16[264,2048]{1,0:T(8,128)(2,1)S(1)}, u32[]{:S(2)}, u32[]{:S(2)}) collective-permute-start(bf16[264,2048]{1,0:T(8,128)(2,1)S(1)} %collective-permute-done.3.refs_4_.refs_0_.refs_2_.refs_6_.refs_8_), channel_id=1, source_target_pairs={{0,4},{4,0},{8,12},{12,8},{16,20},{20,16},{24,28},{28,24},{1,5},{5... | collective-permute-start | bytes 3244040 | tf_op jit(solution)/shard_map/ppermute | solution.py:21
  89.9 12.0 %collective-permute-start.22 = (bf16[256,1024]{1,0:T(8,128)(2,1)}, bf16[256,1024]{1,0:T(8,128)(2,1)S(1)}, u32[]{:S(2)}, u32[]{:S(2)}) collective-permute-start(bf16[256,1024]{1,0:T(8,128)(2,1)} %get-tuple-element.93), channel_id=1, source_target_pairs={{0,4},{4,0},{8,12},{12,8},{16,20},{20,16},{24,28},{28,24},{1,5},{5... | collective-permute-start | bytes 1572872 | tf_op jit(solution)/shard_map/ppermute | solution.py:21
  90.2 14.3 %collective-permute-start.25 = (bf16[256,1024]{1,0:T(8,128)(2,1)S(1)}, bf16[256,1024]{1,0:T(8,128)(2,1)S(1)}, u32[]{:S(2)}, u32[]{:S(2)}) collective-permute-start(bf16[256,1024]{1,0:T(8,128)(2,1)S(1)} %add_convert_fusion.5.refs_18_), channel_id=1, source_target_pairs={{0,8},{4,12},{8,0},{12,4},{16,24},{20,28},{24,16},{28,20},{1,9},{5... | collective-permute-start | bytes 1572872 | tf_op jit(solution)/shard_map/ppermute | solution.py:21
  101.0 30.0 %collective-permute-start.21 = (bf16[256,1024]{1,0:T(8,128)(2,1)}, bf16[256,1024]{1,0:T(8,128)(2,1)}, u32[]{:S(2)}, u32[]{:S(2)}) collective-permute-start(bf16[256,1024]{1,0:T(8,128)(2,1)} %get-tuple-element.91), channel_id=1, source_target_pairs={{0,4},{4,0},{8,12},{12,8},{16,20},{20,16},{24,28},{28,24},{1,5},{5... | collective-permute-start | bytes 1572872 | tf_op jit(solution)/shard_map/ppermute | solution.py:21
  101.4 14.0 %collective-permute-start.16 = (bf16[256,1024]{1,0:T(8,128)(2,1)S(1)}, bf16[256,1024]{1,0:T(8,128)(2,1)S(1)}, u32[]{:S(2)}, u32[]{:S(2)}) collective-permute-start(bf16[256,1024]{1,0:T(8,128)(2,1)S(1)} %add_convert_fusion.7.refs_19_), channel_id=1, source_target_pairs={{0,16},{4,20},{8,24},{12,28},{16,0},{20,4},{24,8},{28,12},{1,17},{... | collective-permute-start | bytes 1572872 | tf_op jit(solution)/shard_map/ppermute | solution.py:21
  101.9 14.0 %collective-permute-start.14 = (bf16[256,1024]{1,0:T(8,128)(2,1)S(1)}, bf16[256,1024]{1,0:T(8,128)(2,1)S(1)}, u32[]{:S(2)}, u32[]{:S(2)}) collective-permute-start(bf16[256,1024]{1,0:T(8,128)(2,1)S(1)} %copy-done.28), channel_id=1, source_target_pairs={{0,4},{4,0},{8,12},{12,8},{16,20},{20,16},{24,28},{28,24},{1,5},{5... | collective-permute-start | bytes 1572872 | tf_op jit(solution)/shard_map/ppermute | solution.py:21
  104.5 13.0 %collective-permute-start.19 = (bf16[256,1024]{1,0:T(8,128)(2,1)S(1)}, bf16[256,1024]{1,0:T(8,128)(2,1)S(1)}, u32[]{:S(2)}, u32[]{:S(2)}) collective-permute-start(bf16[256,1024]{1,0:T(8,128)(2,1)S(1)} %copy-done.29), channel_id=1, source_target_pairs={{0,4},{4,0},{8,12},{12,8},{16,20},{20,16},{24,28},{28,24},{1,5},{5... | collective-permute-start | bytes 1572872 | tf_op jit(solution)/shard_map/ppermute | solution.py:21
  104.5 15.5 %collective-permute-start.23 = (bf16[256,1024]{1,0:T(8,128)(2,1)}, bf16[256,1024]{1,0:T(8,128)(2,1)}, u32[]{:S(2)}, u32[]{:S(2)}) collective-permute-start(bf16[256,1024]{1,0:T(8,128)(2,1)} %add_convert_fusion.3), channel_id=1, source_target_pairs={{0,8},{4,12},{8,0},{12,4},{16,24},{20,28},{24,16},{28,20},{1,9},{5... | collective-permute-start | bytes 1572872 | tf_op jit(solution)/shard_map/ppermute | solution.py:21
  115.3 15.1 %collective-permute-start.26 = (bf16[256,1024]{1,0:T(8,128)(2,1)}, bf16[256,1024]{1,0:T(8,128)(2,1)}, u32[]{:S(2)}, u32[]{:S(2)}) collective-permute-start(bf16[256,1024]{1,0:T(8,128)(2,1)} %add_convert_fusion.2), channel_id=1, source_target_pairs={{0,16},{4,20},{8,24},{12,28},{16,0},{20,4},{24,8},{28,12},{1,17},{... | collective-permute-start | bytes 1572872 | tf_op jit(solution)/shard_map/ppermute | solution.py:21
  117.0 16.4 %collective-permute-start.17 = (bf16[256,1024]{1,0:T(8,128)(2,1)}, bf16[256,1024]{1,0:T(8,128)(2,1)}, u32[]{:S(2)}, u32[]{:S(2)}) collective-permute-start(bf16[256,1024]{1,0:T(8,128)(2,1)} %add_convert_fusion.6), channel_id=1, source_target_pairs={{0,8},{4,12},{8,0},{12,4},{16,24},{20,28},{24,16},{28,20},{1,9},{5... | collective-permute-start | bytes 1572872 | tf_op jit(solution)/shard_map/ppermute | solution.py:21
  118.5 25.8 %collective-permute-start.20 = (bf16[256,1024]{1,0:T(8,128)(2,1)}, bf16[256,1024]{1,0:T(8,128)(2,1)}, u32[]{:S(2)}, u32[]{:S(2)}) collective-permute-start(bf16[256,1024]{1,0:T(8,128)(2,1)} %add_convert_fusion.4), channel_id=1, source_target_pairs={{0,16},{4,20},{8,24},{12,28},{16,0},{20,4},{24,8},{28,12},{1,17},{... | collective-permute-start | bytes 1572872 | tf_op jit(solution)/shard_map/ppermute | solution.py:21
  120.0 28.5 %collective-permute-start.7 = (bf16[256,1024]{1,0:T(8,128)(2,1)}, bf16[256,1024]{1,0:T(8,128)(2,1)S(1)}, u32[]{:S(2)}, u32[]{:S(2)}) collective-permute-start(bf16[256,1024]{1,0:T(8,128)(2,1)} %get-tuple-element.73), channel_id=1, source_target_pairs={{0,4},{4,0},{8,12},{12,8},{16,20},{20,16},{24,28},{28,24},{1,5},{5... | collective-permute-start | bytes 1572872 | tf_op jit(solution)/shard_map/ppermute | solution.py:21
  130.5 15.5 %collective-permute-start.33 = (bf16[4,128,128]{2,1,0:T(8,128)(2,1)S(1)}, bf16[4,128,128]{2,1,0:T(8,128)(2,1)S(1)}, u32[]{:S(2)}, u32[]{:S(2)}) collective-permute-start(bf16[4,128,128]{2,1,0:T(8,128)(2,1)S(1)} %forward_states.1), channel_id=1, source_target_pairs={{0,8},{4,12},{8,0},{12,4},{16,24},{20,28},{24,16},{28,20},{1,9},{5... | collective-permute-start | bytes 393224 | tf_op jit(solution)/shard_map/ppermute | solution.py:21
  131.0 19.5 %collective-permute-start.34 = (bf16[4,128,128]{2,1,0:T(8,128)(2,1)S(1)}, bf16[4,128,128]{2,1,0:T(8,128)(2,1)S(1)}, u32[]{:S(2)}, u32[]{:S(2)}) collective-permute-start(bf16[4,128,128]{2,1,0:T(8,128)(2,1)S(1)} %forward_states.1), channel_id=1, source_target_pairs={{0,16},{4,20},{8,24},{12,28},{16,0},{20,4},{24,8},{28,12},{1,17},{... | collective-permute-start | bytes 393224 | tf_op jit(solution)/shard_map/ppermute | solution.py:21
  133.3 17.2 %collective-permute-start.35 = (bf16[4,128,128]{2,1,0:T(8,128)(2,1)S(1)}, bf16[4,128,128]{2,1,0:T(8,128)(2,1)S(1)}, u32[]{:S(2)}, u32[]{:S(2)}) collective-permute-start(bf16[4,128,128]{2,1,0:T(8,128)(2,1)S(1)} %forward_states.1), channel_id=1, source_target_pairs={{0,24},{4,28},{8,16},{12,20},{16,8},{20,12},{24,0},{28,4},{1,25},{... | collective-permute-start | bytes 393224 | tf_op jit(solution)/shard_map/ppermute | solution.py:21
  146.0 10.2 %collective-permute-start.31 = (bf16[256,256]{1,0:T(8,128)(2,1)S(1)}, bf16[256,256]{1,0:T(8,128)(2,1)S(1)}, u32[]{:S(2)}, u32[]{:S(2)}) collective-permute-start(bf16[256,256]{1,0:T(8,128)(2,1)S(1)} %get-tuple-element.133), channel_id=1, source_target_pairs={{0,2},{1,3},{2,0},{3,1},{4,6},{5,7},{6,4},{7,5},{8,10},{9,11},{10,... | collective-permute-start | bytes 393224 | tf_op jit(solution)/shard_map/ppermute | solution.py:21
  151.1 10.1 %collective-permute-start.38 = (bf16[4,128,128]{2,1,0:T(8,128)(2,1)S(1)}, bf16[4,128,128]{2,1,0:T(8,128)(2,1)S(1)}, u32[]{:S(2)}, u32[]{:S(2)}) collective-permute-start(bf16[4,128,128]{2,1,0:T(8,128)(2,1)S(1)} %collective-permute-done.34.refs_3_), channel_id=1, source_target_pairs={{0,4},{4,0},{8,12},{12,8},{16,20},{20,16},{24,28},{28,24},{1,5},{5... | collective-permute-start | bytes 393224 | tf_op jit(solution)/shard_map/ppermute | solution.py:21
  158.5 12.3 %collective-permute-start.28 = (bf16[256,256]{1,0:T(8,128)(2,1)S(1)}, bf16[256,256]{1,0:T(8,128)(2,1)S(1)}, u32[]{:S(2)}, u32[]{:S(2)}) collective-permute-start(bf16[256,256]{1,0:T(8,128)(2,1)S(1)} %get-tuple-element.136), channel_id=1, source_target_pairs={{0,2},{1,3},{2,0},{3,1},{4,6},{5,7},{6,4},{7,5},{8,10},{9,11},{10,... | collective-permute-start | bytes 393224 | tf_op jit(solution)/shard_map/ppermute | solution.py:21
  159.8 10.9 %collective-permute-start.29 = (bf16[256,256]{1,0:T(8,128)(2,1)S(1)}, bf16[256,256]{1,0:T(8,128)(2,1)S(1)}, u32[]{:S(2)}, u32[]{:S(2)}) collective-permute-start(bf16[256,256]{1,0:T(8,128)(2,1)S(1)} %get-tuple-element.135), channel_id=1, source_target_pairs={{0,3},{1,2},{2,1},{3,0},{4,7},{5,6},{6,5},{7,4},{8,11},{9,10},{10,... | collective-permute-start | bytes 393224 | tf_op jit(solution)/shard_map/ppermute | solution.py:21
  171.5 12.3 %collective-permute-start.43 = (bf16[2,128,128]{2,1,0:T(8,128)(2,1)S(1)}, bf16[2,128,128]{2,1,0:T(8,128)(2,1)S(1)}, u32[]{:S(2)}, u32[]{:S(2)}) collective-permute-start(bf16[2,128,128]{2,1,0:T(8,128)(2,1)S(1)} %get-tuple-element.118), channel_id=1, source_target_pairs={{0,16},{4,20},{8,24},{12,28},{16,0},{20,4},{24,8},{28,12},{1,17},{... | collective-permute-start | bytes 196616 | tf_op jit(solution)/shard_map/ppermute | solution.py:21
  171.7 12.1 %collective-permute-start.48 = (bf16[2,128,128]{2,1,0:T(8,128)(2,1)S(1)}, bf16[2,128,128]{2,1,0:T(8,128)(2,1)S(1)}, u32[]{:S(2)}, u32[]{:S(2)}) collective-permute-start(bf16[2,128,128]{2,1,0:T(8,128)(2,1)S(1)} %get-tuple-element.103), channel_id=1, source_target_pairs={{0,8},{4,12},{8,0},{12,4},{16,24},{20,28},{24,16},{28,20},{1,9},{5... | collective-permute-start | bytes 196616 | tf_op jit(solution)/shard_map/ppermute | solution.py:21
  173.7 10.7 %collective-permute-start.50 = (bf16[2,128,128]{2,1,0:T(8,128)(2,1)S(1)}, bf16[2,128,128]{2,1,0:T(8,128)(2,1)S(1)}, u32[]{:S(2)}, u32[]{:S(2)}) collective-permute-start(bf16[2,128,128]{2,1,0:T(8,128)(2,1)S(1)} %get-tuple-element.103), channel_id=1, source_target_pairs={{0,16},{4,20},{8,24},{12,28},{16,0},{20,4},{24,8},{28,12},{1,17},{... | collective-permute-start | bytes 196616 | tf_op jit(solution)/shard_map/ppermute | solution.py:21
  (59 other events, 478.9 us)

commit v3 on v2

--- a/solution.py
+++ b/solution.py
@@ -147,7 +147,6 @@
             flops=4 * m * width * (3 * ffp + 2 * tok), transcendentals=m * ffp, bytes_accessed=4 * m * width
         ),
         compiler_params=pltpu.CompilerParams(vmem_limit_bytes=(4 + 13 * count) << 20),
-        name="expert_group",
     )(
         scal,
         *[load[0][0] for load in loads],
@@ -200,7 +199,6 @@
         out_shape=jax.ShapeDtypeStruct((heads, HEAD_DIM, HEAD_DIM), BF16),
         cost_estimate=small_cost(1),
         compiler_params=pltpu.CompilerParams(vmem_limit_bytes=8 << 20),
-        name="forward_states",
     )(seg_col, left, right)
 
 
@@ -228,7 +226,6 @@
         ],
         cost_estimate=small_cost(1),
         compiler_params=pltpu.CompilerParams(vmem_limit_bytes=8 << 20),
-        name="backward_states",
     )(place[None], seg_col, left, total, *pieces)
 
 
@@ -304,7 +301,6 @@
         input_output_aliases={6 + shards: 0} if filled else {},
         cost_estimate=small_cost(3),
         compiler_params=pltpu.CompilerParams(vmem_limit_bytes=8 << 20),
-        name="inner_grads",
     )(weights, seg_col, seg_row, q, k, v, g, *states, *filled)
 
 
@@ -331,7 +327,6 @@
         input_output_aliases={5 + shards: 0, 6 + shards: 1} if filled else {},
         cost_estimate=small_cost(2),
         compiler_params=pltpu.CompilerParams(vmem_limit_bytes=8 << 20),
-        name="outer_grads",
     )(weights, seg_col, k, v, dk, dv, *states, *filled)
 
 
@@ -376,7 +371,6 @@
         ),
         out_shape=[jax.ShapeDtypeStruct(x, t) for x, t in zip(shapes, (BF16, BF16, BF16, F32, F32))],
         cost_estimate=small_cost(2),
-        name="make_load",
     )(parity[None], rows, gates, ids, seg)
 
 
@@ -416,7 +410,6 @@
         out_shape=jax.ShapeDtypeStruct((8, 128), F32),
         cost_estimate=small_cost(1),
         compiler_params=pltpu.CompilerParams(vmem_limit_bytes=8 << 20),
-        name="state_weights",
     )(me[None], *[x for x, b in loads])
 
 
@@ -443,7 +436,10 @@
     expert = 2 * me + place // (groups // 2)
     corners = [3] if chips == 4 else []
     sides = [j for j in range(1, chips) if j not in corners]
-    weights3 = [pltpu.with_memory_space_constraint(x[0], pltpu.VMEM) for x in (w_down, w_gate, w_up)]
+    far_weights, weights3 = (
+        [pltpu.with_memory_space_constraint(x[0], space) for x in (w_down, w_gate, w_up)]
+        for space in (pltpu.HBM, pltpu.VMEM)
+    )
 
     load, low, high, seg_col, seg_row = make_load(
         parity, out_grad, gate_values.T, expert_ids.T, segment_ids[None, :]
@@ -467,7 +463,7 @@
             loads += [near[j], far[j]]
             sources += [1 + 2 * j, 2 + 2 * j]
         low, high, cot, hidden, token = expert_group(
-            scal, sources, order, tokens, loads, gate_pre[0], up_pre[0], weights3, groups
+            scal, sources, order, tokens, loads, gate_pre[0], up_pre[0], weights3 if tokens else far_weights, groups
         )
         cots.append(cot)
         hiddens.append(hidden)
@@ -492,7 +488,7 @@
     token = experts([0], straight, [])
     for j in corners:
         token = experts([j], turned, token)
-    extra = {}
+    extra, early = {}, {}
     for i, j in enumerate(sides):
         token = experts([j], straight, token)
         if i == 0:
@@ -500,15 +496,26 @@
                 rows = [added(lax.optimization_barrier((*x, *token))[:2]) for x in sums[k]]
                 extra[2] = ([swap(rows[0], "ctx", 2 * 1)], [])
                 extra[1] = ([], [swap(rows[1], "ctx", 2 * 2)])
-                token = [*token, *rows]
+                ready = added(lax.optimization_barrier((*sums[1][0], *rows))[:2])
+                early[1] = swap(ready, "ctx", 2)
+                token = [*token, *rows, ready]
     loads = [(near if r % 2 == 0 else far)[r // 2][1] for r in range(shards)]
     weights = state_weights(me, [(x, b * (width // 4)) for x, b in loads], tok)
 
     part = width // (2 * groups)
-    totals, spreads = [], []
+    totals, spreads, rows = [], [], []
     for c in range(2):
-        rows = [added(sums[j][c] + extra.get(j, ([], []))[c]) for j in sides]
-        sends = [swap(x, "ctx", 2 * j) for j, x in zip(sides, rows)]
+        sends = []
+        for j in sides:
+            if c == 0 and j in early:
+                sends.append(early[j])
+            else:
+                parts = sums[j][c] + extra.get(j, ([], []))[c]
+                row = added(lax.optimization_barrier((*parts, *rows))[: len(parts)])
+                sends.append(swap(row, "ctx", 2 * j))
+                if c == 0:
+                    last = row
+        rows = [last]
         total = sums[0][c][0].astype(F32) + sums[0][c][1].astype(F32)
         sends = lax.optimization_barrier((*sends, *totals))[: len(sides)]
         for x in sends:
@@ -522,17 +529,18 @@
         spreads.append(pieces)
     down_grad = dot(jnp.concatenate(hiddens), jnp.concatenate(cots), (0, 0))
 
-    fwd = all_states(lax.optimization_barrier((*fwd_near, totals[1]))[:chips])
     dq, dk_dv, before = None, [], [totals[1]]
     for c in range(2):
         pieces = lax.optimization_barrier((*spreads[c], *before))[: groups - 1]
         head_cot, own = backward_states(place, seg_col, queries, totals[c], pieces, c, 2)
+        if c == 0:
+            fwd = all_states(lax.optimization_barrier((*fwd_near, own))[:chips])
         back = all_states(near_states(own, chips))
         dq, dk, dv = inner_grads(
             weights, seg_col, seg_row, queries, keys, values, head_cot, fwd, c, 2, dq
         )
+        dk_dv = outer_grads(weights, seg_col, keys, values, dk, dv, back, c, 2, dk_dv)
         before = [own, dk]
-        dk_dv = outer_grads(weights, seg_col, keys, values, dk, dv, back, c, 2, dk_dv)
     return (dq, *dk_dv, down_grad[None])
 
 

time: 190 us -> 182 us (0.958)
  waiting for transfers between devices: 83.3 us -> 76.5 us
    ppermute x54, waiting for transfers between devices: 83.3 us -> 76.5 us  [swap(): lax.ppermute(x, axis, [(i, i ^ offset) for i in range(lax.axis_size(axis))])]
  transfers between devices with their start and end apart: 54 -> 54, of which waited for: 11 -> 13; matrix products, arithmetic and copies ran while one was open for 7% -> 8% of each run, Pallas kernels for 21% -> 22%
where the time goes in v3:
time: 182 us; the launch traced here: 181 us
  waiting for transfers between devices  76.5 us (42%)
  Pallas kernels  44.2 us (24%)
  starting transfers between devices  38.3 us (21%)
  other arithmetic  8.4 us (5%)
  local copies, waits for them, and re-layouts  7.03 us (4%)
  matrix products  5.49 us (3%)
    ppermute x54, waiting for transfers between devices, swap(): lax.ppermute(x, axis, [(i, i ^ offset) for i in range(lax.axis_size(axis))])  76.5 us
    ppermute x54, starting transfers between devices, swap(): lax.ppermute(x, axis, [(i, i ^ offset) for i in range(lax.axis_size(axis))])  38.3 us
    pallas_call x4, Pallas kernels, expert_group(): pl.pallas_call(functools.partial(expert_kernel, count=count, skip=len(tok...  35.5 us
    unnamed x74, local copies, waits for them, and re-layouts  6.84 us
    dot_general x1, matrix products, dot(): lax.dot_general(a, b, ((dims[:1], dims[1:]), ((), ())), preferred_element...  5.49 us
    convert_element_type x6, other arithmetic, added(): return sum((x.astype(F32) for x in xs)).astype(BF16)  4.81 us
  transfers between devices with their start and end apart: 54, of which 13 were waited for; matrix products, arithmetic and copies ran while one was open for 8% of the time, Pallas kernels for 22%

profile of v3, /device:TPU:0, one launch (start us, length us, event | category | flops | bytes accessed | tf_op | source)
XLA Modules:
  0.0 181.1 jit_solution(15166298980885733241)
XLA Ops:
  0.6 2.5 %shard_map.147 = (bf16[264,2048]{1,0:T(8,128)(2,1)}, bf16[264,512]{1,0:T(8,128)(2,1)}, bf16[264,512]{1,0:T(8,128)(2,1)}, f32[256,1]{1,0:T(8,128)}, f32[1,256]{1,0:T(1,128)}) custom-call(s32[1]{0:T(128)} %bitcast.1.scal, bf16[256,2048]{1,0:T(8,128)(2,1)} %rows.1, bf16[8,256]{1,0:T(8,128)(2,1)} %bitcast.51, s32[8,256]{1,0:T(8,128)} %bitcast.50, s32[1,256]{1,0:T(1,128)} %bitcast.52), custom_call_target="tpu_custom_call" | custom-call | flops 1400000000 | bytes 65536 | tf_op jit(solution)/shard_map/pallas_call | solution.py:364
  3.6 2.5 %collective-permute-start.1 = (bf16[264,2048]{1,0:T(8,128)(2,1)}, bf16[264,2048]{1,0:T(8,128)(2,1)S(1)}, u32[]{:S(2)}, u32[]{:S(2)}) collective-permute-start(bf16[264,2048]{1,0:T(8,128)(2,1)} %get-tuple-element.78.refs_0_.refs_2_.refs_4_.refs_6_.refs_8_), channel_id=1, source_target_pairs={{0,8},{4,12},{8,0},{12,4},{16,24},{20,28},{24,16},{28,20},{1,9},{5... | collective-permute-start | bytes 3244040 | tf_op jit(solution)/shard_map/ppermute | solution.py:21
  6.1 1.5 collective-permute-start.5
  9.0 29.3 %collective-permute-done.5.refs_6_.refs_4_ = bf16[264,512]{1,0:T(8,128)(2,1)S(1)} collective-permute-done((bf16[264,512]{1,0:T(8,128)(2,1)}, bf16[264,512]{1,0:T(8,128)(2,1)S(1)}, u32[]{:S(2)}, u32[]{:S(2)}) %collective-permute-start.5) | collective-permute-done | bytes 270368 | tf_op jit(solution)/shard_map/ppermute | solution.py:21
  38.3 5.4 %collective-permute-done.8.refs_0_.refs_2_ = bf16[264,512]{1,0:T(8,128)(2,1)} collective-permute-done((bf16[264,512]{1,0:T(8,128)(2,1)}, bf16[264,512]{1,0:T(8,128)(2,1)}, u32[]{:S(2)}, u32[]{:S(2)}) %collective-permute-start.8) | collective-permute-done | bytes 270368 | tf_op jit(solution)/shard_map/ppermute | solution.py:21
  43.7 1.6 collective-permute-start.10
  46.8 6.6 %collective-permute-done.10.refs_6_ = bf16[264,512]{1,0:T(8,128)(2,1)} collective-permute-done((bf16[264,512]{1,0:T(8,128)(2,1)}, bf16[264,512]{1,0:T(8,128)(2,1)}, u32[]{:S(2)}, u32[]{:S(2)}) %collective-permute-start.10) | collective-permute-done | bytes 270368 | tf_op jit(solution)/shard_map/ppermute | solution.py:21
  53.4 4.5 %collective-permute-done.12.refs_8_ = bf16[264,512]{1,0:T(8,128)(2,1)} collective-permute-done((bf16[264,512]{1,0:T(8,128)(2,1)S(1)}, bf16[264,512]{1,0:T(8,128)(2,1)}, u32[]{:S(2)}, u32[]{:S(2)}) %collective-permute-start.12) | collective-permute-done | bytes 270368 | tf_op jit(solution)/shard_map/ppermute | solution.py:21
  58.5 1.6 copy-done.3
  60.0 9.5 %shard_map.149 = (bf16[256,1024]{1,0:T(8,128)(2,1)}, bf16[256,1024]{1,0:T(8,128)(2,1)}, bf16[256,1024]{1,0:T(8,128)(2,1)}, bf16[256,1024]{1,0:T(8,128)(2,1)}, bf...) custom-call(s32[13]{0:T(128)S(1)} %stack.41.scal, bf16[264,2048]{1,0:T(8,128)(2,1)S(1)} %copy-done.3, ...), custom_call_target="tpu_custom_call" | custom-call | flops 6442450944 | bytes 3145728 | tf_op jit(solution)/shard_map/pallas_call | solution.py:120
  69.6 8.5 %shard_map.150 = (bf16[256,1024]{1,0:T(8,128)(2,1)}, bf16[256,1024]{1,0:T(8,128)(2,1)}, bf16[256,1024]{1,0:T(8,128)(2,1)}, bf16[256,1024]{1,0:T(8,128)(2,1)}, bf...) custom-call(s32[13]{0:T(128)S(1)} %stack.41.scal, ...), custom_call_target="tpu_custom_call" | custom-call | flops 6442450944 | bytes 3145728 | tf_op jit(solution)/shard_map/pallas_call | solution.py:120
  79.0 8.7 %shard_map.151 = (bf16[256,1024]{1,0:T(8,128)(2,1)}, bf16[256,1024]{1,0:T(8,128)(2,1)}, bf16[256,1024]{1,0:T(8,128)(2,1)}, bf16[256,1024]{1,0:T(8,128)(2,1)}, bf...) custom-call(s32[13]{0:T(128)S(1)} %stack.41.scal, ...), custom_call_target="tpu_custom_call" | custom-call | flops 6442450944 | bytes 3145728 | tf_op jit(solution)/shard_map/pallas_call | solution.py:120
  88.2 1.6 collective-permute-start.20
  90.2 8.8 %shard_map.152 = (bf16[256,1024]{1,0:T(8,128)(2,1)}, bf16[256,1024]{1,0:T(8,128)(2,1)}, bf16[256,1024]{1,0:T(8,128)(2,1)}, bf16[256,1024]{1,0:T(8,128)(2,1)}, bf...) custom-call(s32[13]{0:T(128)S(1)} %stack.41.scal, ...), custom_call_target="tpu_custom_call" | custom-call | flops 6442450944 | bytes 3145728 | tf_op jit(solution)/shard_map/pallas_call | solution.py:120
  100.0 2.4 %collective-permute-done.20 = bf16[256,1024]{1,0:T(8,128)(2,1)S(1)} collective-permute-done((bf16[256,1024]{1,0:T(8,128)(2,1)S(1)}, bf16[256,1024]{1,0:T(8,128)(2,1)S(1)}, u32[]{:S(2)}, u32[]{:S(2)}) %collective-permute-start.20) | collective-permute-done | bytes 524320 | tf_op jit(solution)/shard_map/ppermute | solution.py:21
  102.4 1.5 collective-permute-start.25
  103.9 2.1 %add_convert_fusion.4 = bf16[256,1024]{1,0:T(8,128)(2,1)} fusion(bf16[256,1024]{1,0:T(8,128)(2,1)S(1)} %collective-permute-done.20, bf16[256,1024]{1,0:T(8,128)(2,1)S(1)} %collective-permute-done.19, bf16[256,1024]{1,0:T(8,128)(2,1)} %get-tuple-element.104), kind=kLoop, calls=%fused_computation.20 | loop fusion | flops 1572864 | bytes 2097152 | tf_op jit(solution)/shard_map/convert_element_type | solution.py:475
  106.5 7.7 %collective-permute-done.16 = bf16[256,1024]{1,0:T(8,128)(2,1)S(1)} collective-permute-done((bf16[256,1024]{1,0:T(8,128)(2,1)S(1)}, bf16[256,1024]{1,0:T(8,128)(2,1)S(1)}, u32[]{:S(2)}, u32[]{:S(2)}) %collective-permute-start.16) | collective-permute-done | bytes 524320 | tf_op jit(solution)/shard_map/ppermute | solution.py:21
  123.5 2.2 %collective-permute-done.26 = bf16[256,1024]{1,0:T(8,128)(2,1)} collective-permute-done((bf16[256,1024]{1,0:T(8,128)(2,1)}, bf16[256,1024]{1,0:T(8,128)(2,1)}, u32[]{:S(2)}, u32[]{:S(2)}) %collective-permute-start.26) | collective-permute-done | bytes 524320 | tf_op jit(solution)/shard_map/ppermute | solution.py:21
  127.6 1.9 %add_convert_fusion.1.refs_0_ = bf16[256,1024]{1,0:T(8,128)(2,1)S(1)} fusion(bf16[256,1024]{1,0:T(8,128)(2,1)} %collective-permute-done.26, bf16[256,1024]{1,0:T(8,128)(2,1)} %collective-permute-done.25, bf16[256,1024]{1,0:T(8,128)(2,1)} %collective-permute-done.24, bf16[256,1024]{1,0:T(8,128)(2,1)S(1)} %copy-done.22), kind=kLoop, calls=%fused_computation.17 | loop fusion | flops 2097152 | bytes 2621440 | tf_op jit(solution)/shard_map/convert_element_type | solution.py:523
  129.5 7.4 %collective-permute-done.23 = bf16[256,1024]{1,0:T(8,128)(2,1)} collective-permute-done((bf16[256,1024]{1,0:T(8,128)(2,1)}, bf16[256,1024]{1,0:T(8,128)(2,1)}, u32[]{:S(2)}, u32[]{:S(2)}) %collective-permute-start.23) | collective-permute-done | bytes 524320 | tf_op jit(solution)/shard_map/ppermute | solution.py:21
  136.9 1.6 collective-permute-start.30
  138.5 2.6 %collective-permute-start.31 = (bf16[256,256]{1,0:T(8,128)(2,1)S(1)}, bf16[256,256]{1,0:T(8,128)(2,1)S(1)}, u32[]{:S(2)}, u32[]{:S(2)}) collective-permute-start(bf16[256,256]{1,0:T(8,128)(2,1)S(1)} %get-tuple-element.153), channel_id=1, source_target_pairs={{0,2},{1,3},{2,0},{3,1},{4,6},{5,7},{6,4},{7,5},{8,10},{9,11},{10,... | collective-permute-start | bytes 393224 | tf_op jit(solution)/shard_map/ppermute | solution.py:21
  141.4 1.7 add_convert_fusion.refs_0_
  144.7 5.3 %collective-permute-done.31.refs_2_ = bf16[256,256]{1,0:T(8,128)(2,1)S(1)} collective-permute-done((bf16[256,256]{1,0:T(8,128)(2,1)S(1)}, bf16[256,256]{1,0:T(8,128)(2,1)S(1)}, u32[]{:S(2)}, u32[]{:S(2)}) %collective-permute-start.31) | collective-permute-done | bytes 131104 | tf_op jit(solution)/shard_map/ppermute | solution.py:21
  151.6 5.5 %fusion.8 = f32[1,512,2048]{2,1,0:T(8,128)} fusion(bf16[384,2048]{1,0:T(8,128)(2,1)S(1)} %copy-done.28, bf16[384,2048]{1,0:T(8,128)(2,1)S(1)} %copy-done.31, bf16[384,2048]{1,0:T(8,128)(2,1)S(1)} %copy-done.35, bf16[384,2048]{1,0:T(8,128)(2,1)S(1)} %copy-done.32, bf16[384,512]{1,0:T(8,128)(2,1)S(1)} %copy-done.30, bf16[384,512]{1,0:T(8,128)(2,1)S(1)} %copy-done.33, ...), kind=kOutput, calls=%fused_computation.8 | convolution fusion | flops 3252682752 | bytes 12058624 | tf_op jit(solution)/shard_map/dot_general | solution.py:17
  157.1 3.1 %collective-permute-start.28 = (bf16[256,256]{1,0:T(8,128)(2,1)S(1)}, bf16[256,256]{1,0:T(8,128)(2,1)S(1)}, u32[]{:S(2)}, u32[]{:S(2)}) collective-permute-start(bf16[256,256]{1,0:T(8,128)(2,1)S(1)} %get-tuple-element.156), channel_id=1, source_target_pairs={{0,2},{1,3},{2,0},{3,1},{4,6},{5,7},{6,4},{7,5},{8,10},{9,11},{10,... | collective-permute-start | bytes 393224 | tf_op jit(solution)/shard_map/ppermute | solution.py:21
  161.5 1.5 collective-permute-start.48
  163.5 1.5 collective-permute-start.52
  166.4 3.7 %collective-permute-done.28.refs_2_ = bf16[256,256]{1,0:T(8,128)(2,1)S(1)} collective-permute-done((bf16[256,256]{1,0:T(8,128)(2,1)S(1)}, bf16[256,256]{1,0:T(8,128)(2,1)S(1)}, u32[]{:S(2)}, u32[]{:S(2)}) %collective-permute-start.28) | collective-permute-done | bytes 131104 | tf_op jit(solution)/shard_map/ppermute | solution.py:21
  171.5 1.6 collective-permute-start.41
  173.6 1.5 collective-permute-start.45
  (175 shorter events, 32.9 us)
Async XLA Ops:
  3.1 54.8 %collective-permute-start = (bf16[264,2048]{1,0:T(8,128)(2,1)}, bf16[264,2048]{1,0:T(8,128)(2,1)S(1)}, u32[]{:S(2)}, u32[]{:S(2)}) collective-permute-start(bf16[264,2048]{1,0:T(8,128)(2,1)} %get-tuple-element.78.refs_0_.refs_2_.refs_4_.refs_6_.refs_8_), channel_id=1, source_target_pairs={{0,4},{4,0},{8,12},{12,8},{16,20},{20,16},{24,28},{28,24},{1,5},{5... | collective-permute-start | bytes 3244040 | tf_op jit(solution)/shard_map/ppermute | solution.py:21
  3.6 54.8 %collective-permute-start.1 = (bf16[264,2048]{1,0:T(8,128)(2,1)}, bf16[264,2048]{1,0:T(8,128)(2,1)S(1)}, u32[]{:S(2)}, u32[]{:S(2)}) collective-permute-start(bf16[264,2048]{1,0:T(8,128)(2,1)} %get-tuple-element.78.refs_0_.refs_2_.refs_4_.refs_6_.refs_8_), channel_id=1, source_target_pairs={{0,8},{4,12},{8,0},{12,4},{16,24},{20,28},{24,16},{28,20},{1,9},{5... | collective-permute-start | bytes 3244040 | tf_op jit(solution)/shard_map/ppermute | solution.py:21
  6.1 32.2 %collective-permute-start.5 = (bf16[264,512]{1,0:T(8,128)(2,1)}, bf16[264,512]{1,0:T(8,128)(2,1)S(1)}, u32[]{:S(2)}, u32[]{:S(2)}) collective-permute-start(bf16[264,512]{1,0:T(8,128)(2,1)} %get-tuple-element.79), channel_id=1, source_target_pairs={{0,24},{4,28},{8,16},{12,20},{16,8},{20,12},{24,0},{28,4},{1,25},{... | collective-permute-start | bytes 811016 | tf_op jit(solution)/shard_map/ppermute | solution.py:21
  7.6 36.1 %collective-permute-start.8 = (bf16[264,512]{1,0:T(8,128)(2,1)}, bf16[264,512]{1,0:T(8,128)(2,1)}, u32[]{:S(2)}, u32[]{:S(2)}) collective-permute-start(bf16[264,512]{1,0:T(8,128)(2,1)} %get-tuple-element.84), channel_id=1, source_target_pairs={{0,24},{4,28},{8,16},{12,20},{16,8},{20,12},{24,0},{28,4},{1,25},{... | collective-permute-start | bytes 811016 | tf_op jit(solution)/shard_map/ppermute | solution.py:21
  43.7 9.7 %collective-permute-start.10 = (bf16[264,512]{1,0:T(8,128)(2,1)}, bf16[264,512]{1,0:T(8,128)(2,1)}, u32[]{:S(2)}, u32[]{:S(2)}) collective-permute-start(bf16[264,512]{1,0:T(8,128)(2,1)} %collective-permute-done.8.refs_0_.refs_2_), channel_id=1, source_target_pairs={{0,1},{1,0},{2,3},{3,2},{4,5},{5,4},{6,7},{7,6},{8,9},{9,8},{10,11... | collective-permute-start | bytes 811016 | tf_op jit(solution)/shard_map/ppermute | solution.py:21
  45.3 12.6 %collective-permute-start.12 = (bf16[264,512]{1,0:T(8,128)(2,1)S(1)}, bf16[264,512]{1,0:T(8,128)(2,1)}, u32[]{:S(2)}, u32[]{:S(2)}) collective-permute-start(bf16[264,512]{1,0:T(8,128)(2,1)S(1)} %collective-permute-done.5.refs_6_.refs_4_), channel_id=1, source_target_pairs={{0,1},{1,0},{2,3},{3,2},{4,5},{5,4},{6,7},{7,6},{8,9},{9,8},{10,11... | collective-permute-start | bytes 811016 | tf_op jit(solution)/shard_map/ppermute | solution.py:21
  46.6 32.1 %collective-permute-start.3 = (bf16[264,2048]{1,0:T(8,128)(2,1)}, bf16[264,2048]{1,0:T(8,128)(2,1)S(1)}, u32[]{:S(2)}, u32[]{:S(2)}) collective-permute-start(bf16[264,2048]{1,0:T(8,128)(2,1)} %get-tuple-element.78.refs_0_.refs_2_.refs_4_.refs_6_.refs_8_), channel_id=1, source_target_pairs={{0,16},{4,20},{8,24},{12,28},{16,0},{20,4},{24,8},{28,12},{1,17},{... | collective-permute-start | bytes 3244040 | tf_op jit(solution)/shard_map/ppermute | solution.py:21
  53.4 16.2 %collective-permute-start.9 = (bf16[264,512]{1,0:T(8,128)(2,1)}, bf16[264,512]{1,0:T(8,128)(2,1)S(1)}, u32[]{:S(2)}, u32[]{:S(2)}) collective-permute-start(bf16[264,512]{1,0:T(8,128)(2,1)} %collective-permute-done.8.refs_0_.refs_2_), channel_id=1, source_target_pairs={{0,4},{4,0},{8,12},{12,8},{16,20},{20,16},{24,28},{28,24},{1,5},{5... | collective-permute-start | bytes 811016 | tf_op jit(solution)/shard_map/ppermute | solution.py:21
  57.9 11.7 %collective-permute-start.11 = (bf16[264,512]{1,0:T(8,128)(2,1)}, bf16[264,512]{1,0:T(8,128)(2,1)S(1)}, u32[]{:S(2)}, u32[]{:S(2)}) collective-permute-start(bf16[264,512]{1,0:T(8,128)(2,1)} %collective-permute-done.10.refs_6_), channel_id=1, source_target_pairs={{0,4},{4,0},{8,12},{12,8},{16,20},{20,16},{24,28},{28,24},{1,5},{5... | collective-permute-start | bytes 811016 | tf_op jit(solution)/shard_map/ppermute | solution.py:21
  57.9 11.7 %collective-permute-start.13 = (bf16[264,512]{1,0:T(8,128)(2,1)}, bf16[264,512]{1,0:T(8,128)(2,1)S(1)}, u32[]{:S(2)}, u32[]{:S(2)}) collective-permute-start(bf16[264,512]{1,0:T(8,128)(2,1)} %collective-permute-done.12.refs_8_), channel_id=1, source_target_pairs={{0,4},{4,0},{8,12},{12,8},{16,20},{20,16},{24,28},{28,24},{1,5},{5... | collective-permute-start | bytes 811016 | tf_op jit(solution)/shard_map/ppermute | solution.py:21
  58.4 20.6 %collective-permute-start.2 = (bf16[264,2048]{1,0:T(8,128)(2,1)S(1)}, bf16[264,2048]{1,0:T(8,128)(2,1)S(1)}, u32[]{:S(2)}, u32[]{:S(2)}) collective-permute-start(bf16[264,2048]{1,0:T(8,128)(2,1)S(1)} %collective-permute-done.1.refs_2_.refs_0_.refs_4_.refs_6_.refs_8_), channel_id=1, source_target_pairs={{0,4},{4,0},{8,12},{12,8},{16,20},{20,16},{24,28},{28,24},{1,5},{5... | collective-permute-start | bytes 3244040 | tf_op jit(solution)/shard_map/ppermute | solution.py:21
  78.1 9.5 %collective-permute-start.15 = (bf16[256,1024]{1,0:T(8,128)(2,1)}, bf16[256,1024]{1,0:T(8,128)(2,1)S(1)}, u32[]{:S(2)}, u32[]{:S(2)}) collective-permute-start(bf16[256,1024]{1,0:T(8,128)(2,1)} %get-tuple-element.90), channel_id=1, source_target_pairs={{0,4},{4,0},{8,12},{12,8},{16,20},{20,16},{24,28},{28,24},{1,5},{5... | collective-permute-start | bytes 1572872 | tf_op jit(solution)/shard_map/ppermute | solution.py:21
  78.5 9.2 %collective-permute-start.17 = (bf16[256,1024]{1,0:T(8,128)(2,1)}, bf16[256,1024]{1,0:T(8,128)(2,1)S(1)}, u32[]{:S(2)}, u32[]{:S(2)}) collective-permute-start(bf16[256,1024]{1,0:T(8,128)(2,1)} %get-tuple-element.95), channel_id=1, source_target_pairs={{0,4},{4,0},{8,12},{12,8},{16,20},{20,16},{24,28},{28,24},{1,5},{5... | collective-permute-start | bytes 1572872 | tf_op jit(solution)/shard_map/ppermute | solution.py:21
  78.7 11.5 %collective-permute-start.4 = (bf16[264,2048]{1,0:T(8,128)(2,1)S(1)}, bf16[264,2048]{1,0:T(8,128)(2,1)S(1)}, u32[]{:S(2)}, u32[]{:S(2)}) collective-permute-start(bf16[264,2048]{1,0:T(8,128)(2,1)S(1)} %collective-permute-done.3.refs_4_.refs_0_.refs_2_.refs_6_.refs_8_), channel_id=1, source_target_pairs={{0,4},{4,0},{8,12},{12,8},{16,20},{20,16},{24,28},{28,24},{1,5},{5... | collective-permute-start | bytes 3244040 | tf_op jit(solution)/shard_map/ppermute | solution.py:21
  88.2 14.2 %collective-permute-start.20 = (bf16[256,1024]{1,0:T(8,128)(2,1)S(1)}, bf16[256,1024]{1,0:T(8,128)(2,1)S(1)}, u32[]{:S(2)}, u32[]{:S(2)}) collective-permute-start(bf16[256,1024]{1,0:T(8,128)(2,1)S(1)} %add_convert_fusion.6.refs_18_), channel_id=1, source_target_pairs={{0,8},{4,12},{8,0},{12,4},{16,24},{20,28},{24,16},{28,20},{1,9},{5... | collective-permute-start | bytes 1572872 | tf_op jit(solution)/shard_map/ppermute | solution.py:21
  99.5 14.8 %collective-permute-start.16 = (bf16[256,1024]{1,0:T(8,128)(2,1)S(1)}, bf16[256,1024]{1,0:T(8,128)(2,1)S(1)}, u32[]{:S(2)}, u32[]{:S(2)}) collective-permute-start(bf16[256,1024]{1,0:T(8,128)(2,1)S(1)} %add_convert_fusion.7.refs_19_), channel_id=1, source_target_pairs={{0,16},{4,20},{8,24},{12,28},{16,0},{20,4},{24,8},{28,12},{1,17},{... | collective-permute-start | bytes 1572872 | tf_op jit(solution)/shard_map/ppermute | solution.py:21
  100.0 27.1 %collective-permute-start.24 = (bf16[256,1024]{1,0:T(8,128)(2,1)}, bf16[256,1024]{1,0:T(8,128)(2,1)}, u32[]{:S(2)}, u32[]{:S(2)}) collective-permute-start(bf16[256,1024]{1,0:T(8,128)(2,1)} %get-tuple-element.115), channel_id=1, source_target_pairs={{0,4},{4,0},{8,12},{12,8},{16,20},{20,16},{24,28},{28,24},{1,5},{5... | collective-permute-start | bytes 1572872 | tf_op jit(solution)/shard_map/ppermute | solution.py:21
  102.4 16.0 %collective-permute-start.25 = (bf16[256,1024]{1,0:T(8,128)(2,1)S(1)}, bf16[256,1024]{1,0:T(8,128)(2,1)}, u32[]{:S(2)}, u32[]{:S(2)}) collective-permute-start(bf16[256,1024]{1,0:T(8,128)(2,1)S(1)} %add_convert_fusion.5.refs_20_), channel_id=1, source_target_pairs={{0,8},{4,12},{8,0},{12,4},{16,24},{20,28},{24,16},{28,20},{1,9},{5... | collective-permute-start | bytes 1572872 | tf_op jit(solution)/shard_map/ppermute | solution.py:21
  103.9 12.9 %collective-permute-start.22 = (bf16[256,1024]{1,0:T(8,128)(2,1)}, bf16[256,1024]{1,0:T(8,128)(2,1)S(1)}, u32[]{:S(2)}, u32[]{:S(2)}) collective-permute-start(bf16[256,1024]{1,0:T(8,128)(2,1)} %get-tuple-element.111), channel_id=1, source_target_pairs={{0,4},{4,0},{8,12},{12,8},{16,20},{20,16},{24,28},{28,24},{1,5},{5... | collective-permute-start | bytes 1572872 | tf_op jit(solution)/shard_map/ppermute | solution.py:21
  106.0 19.6 %collective-permute-start.26 = (bf16[256,1024]{1,0:T(8,128)(2,1)}, bf16[256,1024]{1,0:T(8,128)(2,1)}, u32[]{:S(2)}, u32[]{:S(2)}) collective-permute-start(bf16[256,1024]{1,0:T(8,128)(2,1)} %add_convert_fusion.4), channel_id=1, source_target_pairs={{0,16},{4,20},{8,24},{12,28},{16,0},{20,4},{24,8},{28,12},{1,17},{... | collective-permute-start | bytes 1572872 | tf_op jit(solution)/shard_map/ppermute | solution.py:21
  115.4 14.1 %collective-permute-start.21 = (bf16[256,1024]{1,0:T(8,128)(2,1)}, bf16[256,1024]{1,0:T(8,128)(2,1)}, u32[]{:S(2)}, u32[]{:S(2)}) collective-permute-start(bf16[256,1024]{1,0:T(8,128)(2,1)} %add_convert_fusion.3), channel_id=1, source_target_pairs={{0,8},{4,12},{8,0},{12,4},{16,24},{20,28},{24,16},{28,20},{1,9},{5... | collective-permute-start | bytes 1572872 | tf_op jit(solution)/shard_map/ppermute | solution.py:21
  117.8 19.0 %collective-permute-start.23 = (bf16[256,1024]{1,0:T(8,128)(2,1)}, bf16[256,1024]{1,0:T(8,128)(2,1)}, u32[]{:S(2)}, u32[]{:S(2)}) collective-permute-start(bf16[256,1024]{1,0:T(8,128)(2,1)} %add_convert_fusion.2), channel_id=1, source_target_pairs={{0,16},{4,20},{8,24},{12,28},{16,0},{20,4},{24,8},{28,12},{1,17},{... | collective-permute-start | bytes 1572872 | tf_op jit(solution)/shard_map/ppermute | solution.py:21
  118.4 22.7 %collective-permute-start.7 = (bf16[256,1024]{1,0:T(8,128)(2,1)}, bf16[256,1024]{1,0:T(8,128)(2,1)S(1)}, u32[]{:S(2)}, u32[]{:S(2)}) collective-permute-start(bf16[256,1024]{1,0:T(8,128)(2,1)} %get-tuple-element.83), channel_id=1, source_target_pairs={{0,4},{4,0},{8,12},{12,8},{16,20},{20,16},{24,28},{28,24},{1,5},{5... | collective-permute-start | bytes 1572872 | tf_op jit(solution)/shard_map/ppermute | solution.py:21
  125.6 24.7 %collective-permute-start.33 = (bf16[4,128,128]{2,1,0:T(8,128)(2,1)S(1)}, bf16[4,128,128]{2,1,0:T(8,128)(2,1)S(1)}, u32[]{:S(2)}, u32[]{:S(2)}) collective-permute-start(bf16[4,128,128]{2,1,0:T(8,128)(2,1)S(1)} %shard_map.154), channel_id=1, source_target_pairs={{0,8},{4,12},{8,0},{12,4},{16,24},{20,28},{24,16},{28,20},{1,9},{5... | collective-permute-start | bytes 393224 | tf_op jit(solution)/shard_map/ppermute | solution.py:21
  127.1 23.3 %collective-permute-start.34 = (bf16[4,128,128]{2,1,0:T(8,128)(2,1)S(1)}, bf16[4,128,128]{2,1,0:T(8,128)(2,1)S(1)}, u32[]{:S(2)}, u32[]{:S(2)}) collective-permute-start(bf16[4,128,128]{2,1,0:T(8,128)(2,1)S(1)} %shard_map.154), channel_id=1, source_target_pairs={{0,16},{4,20},{8,24},{12,28},{16,0},{20,4},{24,8},{28,12},{1,17},{... | collective-permute-start | bytes 393224 | tf_op jit(solution)/shard_map/ppermute | solution.py:21
  138.5 11.5 %collective-permute-start.31 = (bf16[256,256]{1,0:T(8,128)(2,1)S(1)}, bf16[256,256]{1,0:T(8,128)(2,1)S(1)}, u32[]{:S(2)}, u32[]{:S(2)}) collective-permute-start(bf16[256,256]{1,0:T(8,128)(2,1)S(1)} %get-tuple-element.153), channel_id=1, source_target_pairs={{0,2},{1,3},{2,0},{3,1},{4,6},{5,7},{6,4},{7,5},{8,10},{9,11},{10,... | collective-permute-start | bytes 393224 | tf_op jit(solution)/shard_map/ppermute | solution.py:21
  150.4 9.8 %collective-permute-start.36 = (bf16[4,128,128]{2,1,0:T(8,128)(2,1)S(1)}, bf16[4,128,128]{2,1,0:T(8,128)(2,1)S(1)}, u32[]{:S(2)}, u32[]{:S(2)}) collective-permute-start(bf16[4,128,128]{2,1,0:T(8,128)(2,1)S(1)} %shard_map.154), channel_id=1, source_target_pairs={{0,4},{4,0},{8,12},{12,8},{16,20},{20,16},{24,28},{28,24},{1,5},{5... | collective-permute-start | bytes 393224 | tf_op jit(solution)/shard_map/ppermute | solution.py:21
  150.5 11.0 %collective-permute-start.37 = (bf16[4,128,128]{2,1,0:T(8,128)(2,1)S(1)}, bf16[4,128,128]{2,1,0:T(8,128)(2,1)S(1)}, u32[]{:S(2)}, u32[]{:S(2)}) collective-permute-start(bf16[4,128,128]{2,1,0:T(8,128)(2,1)S(1)} %collective-permute-done.33.refs_1_), channel_id=1, source_target_pairs={{0,4},{4,0},{8,12},{12,8},{16,20},{20,16},{24,28},{28,24},{1,5},{5... | collective-permute-start | bytes 393224 | tf_op jit(solution)/shard_map/ppermute | solution.py:21
  151.0 12.0 %collective-permute-start.38 = (bf16[4,128,128]{2,1,0:T(8,128)(2,1)S(1)}, bf16[4,128,128]{2,1,0:T(8,128)(2,1)S(1)}, u32[]{:S(2)}, u32[]{:S(2)}) collective-permute-start(bf16[4,128,128]{2,1,0:T(8,128)(2,1)S(1)} %collective-permute-done.34.refs_3_), channel_id=1, source_target_pairs={{0,4},{4,0},{8,12},{12,8},{16,20},{20,16},{24,28},{28,24},{1,5},{5... | collective-permute-start | bytes 393224 | tf_op jit(solution)/shard_map/ppermute | solution.py:21
  151.1 12.4 %collective-permute-start.39 = (bf16[4,128,128]{2,1,0:T(8,128)(2,1)S(1)}, bf16[4,128,128]{2,1,0:T(8,128)(2,1)S(1)}, u32[]{:S(2)}, u32[]{:S(2)}) collective-permute-start(bf16[4,128,128]{2,1,0:T(8,128)(2,1)S(1)} %collective-permute-done.35.refs_5_), channel_id=1, source_target_pairs={{0,4},{4,0},{8,12},{12,8},{16,20},{20,16},{24,28},{28,24},{1,5},{5... | collective-permute-start | bytes 393224 | tf_op jit(solution)/shard_map/ppermute | solution.py:21
  157.1 13.0 %collective-permute-start.28 = (bf16[256,256]{1,0:T(8,128)(2,1)S(1)}, bf16[256,256]{1,0:T(8,128)(2,1)S(1)}, u32[]{:S(2)}, u32[]{:S(2)}) collective-permute-start(bf16[256,256]{1,0:T(8,128)(2,1)S(1)} %get-tuple-element.156), channel_id=1, source_target_pairs={{0,2},{1,3},{2,0},{3,1},{4,6},{5,7},{6,4},{7,5},{8,10},{9,11},{10,... | collective-permute-start | bytes 393224 | tf_op jit(solution)/shard_map/ppermute | solution.py:21
  160.2 11.0 %collective-permute-start.29 = (bf16[256,256]{1,0:T(8,128)(2,1)S(1)}, bf16[256,256]{1,0:T(8,128)(2,1)S(1)}, u32[]{:S(2)}, u32[]{:S(2)}) collective-permute-start(bf16[256,256]{1,0:T(8,128)(2,1)S(1)} %get-tuple-element.155), channel_id=1, source_target_pairs={{0,3},{1,2},{2,1},{3,0},{4,7},{5,6},{6,5},{7,4},{8,11},{9,10},{10,... | collective-permute-start | bytes 393224 | tf_op jit(solution)/shard_map/ppermute | solution.py:21
  (59 other events, 431.7 us)
